TPU v7x, 32 devices: a whole 2x2x4 slice. The times are simulated.
32 devices in a mesh: span: 8 (over z, x), wall: 4 (over y, core).
Axes of the slice: x: 2, y: 2, z: 4, core: 2. Of those that a mesh axis runs over, the one named last changes fastest.
Arguments:
- forcing: float32 [768, 16384], P('wall', 'span'), may hold values from -6 to 6
- start: float32 [768, 16384], P('wall', 'span'), may hold values from -2 to 2
- wall_even: float32 [384, 384], replicated, may hold values from -0.3125 to 0.3125
- wall_odd: float32 [384, 384], replicated, may hold values from -0.3125 to 0.3125
- diag_shift: float32 [768, 512], P('wall', 'span'), may hold values from 0.5 to 2
- band_coef: float32 [8, 768, 512], P(None, 'wall', 'span'), may hold values from -2 to 2
- offsets: int32 [8], replicated, may hold values from -128 to 128, as said below
- pattern: int32 [8, 512], P(None, 'span'), may hold values 0 or 1
- block_inv: float32 [768, 192], P('wall'), may hold values from -0.109375 to 0.109375
Outputs:
- solution: float32 [768, 16384], P('wall', 'span')
- residual: float32 [768, 16384], P('wall', 'span')
Inputs may be any that keep to these rules, and one draw needn't show every extreme that they name: `offsets`: every offset lies within 128 spanwise points; in every draw one band has offset 2 * 64 and one has offset -128.
All inputs are finite; a program needn't handle non-finite values. No bound on the sum of `pattern` on one device may be relied on, other than what follows from the above.
Results may differ from a plain program's by a relative error of at most 0.0001.
Values sent between devices are 32-bit elements; how exact they have to be, the bound alone decides.
No kernel may reach another device: no remote copies, remote signals or barrier semaphores. Data moves between devices by JAX's collectives and lax.ppermute only.
A program may use at most 128 MiB of HBM per device.

v0:
```python
import functools

import jax
import jax.numpy as jnp
from jax import lax
from jax.experimental import pallas as pl
from jax.experimental.pallas import tpu as pltpu
from jax.sharding import PartitionSpec as P


SWEEPS = 2
CHUNKS = 2
LANES = 128
HALF = LANES // 2
REACH = 2


def exchange(value, bit):
    count = lax.axis_size("wall")
    return lax.ppermute(value, "wall", [(i, i ^ bit) for i in range(count)])


def partner(value):
    count = lax.axis_size("span")
    return lax.ppermute(value, "span", [(i, i ^ 1) for i in range(count)])


def far(value, first):
    count = lax.axis_size("span")
    pairs = []
    for i in range(count):
        up = (i % 2 == 1) == first
        pairs.append((i, (i + (REACH if up else -REACH)) % count))
    return lax.ppermute(value, "span", pairs)


def params():
    return pltpu.CompilerParams(vmem_limit_bytes=40 << 20)


SMEM = pl.BlockSpec(memory_space=pltpu.SMEM)
VMEM = pl.BlockSpec(memory_space=pltpu.VMEM)


def split_kernel(width, x_ref, *out_refs):
    chunks = len(out_refs)
    cw = width // chunks
    half = cw // 2
    per = LANES // width

    def step(g, _):
        lanes = pl.ds(pl.multiple_of(g * LANES, LANES), LANES)
        top = x_ref[:LANES, lanes].T.reshape(per, width, LANES)
        low = x_ref[LANES:, lanes]
        pair = jnp.concatenate([low, pltpu.roll(low, LANES - half, 1)], 0)
        pair = pair.T.reshape(per, width, LANES)
        here = pl.ds(g * per, per)
        for k, out_ref in enumerate(out_refs):
            out_ref[here, :cw, :] = top[:, k * cw : (k + 1) * cw, :]
            out_ref[here, cw:, :] = pair[:, k * cw : k * cw + half, :]
        return 0

    lax.fori_loop(0, x_ref.shape[1] // LANES, step, 0)


def split(x, chunks, points):
    rows, breadth = x.shape
    width = breadth // points
    cw = width // chunks
    out = jax.ShapeDtypeStruct((points, cw + cw // 2, LANES), x.dtype)
    return pl.pallas_call(
        functools.partial(split_kernel, width),
        out_shape=(out,) * chunks,
        in_specs=[VMEM],
        out_specs=(VMEM,) * chunks,
        compiler_params=params(),
        cost_estimate=pl.CostEstimate(flops=0, bytes_accessed=8 * rows * breadth, transcendentals=0),
        name="split",
    )(x)


def join(width, sol_parts, res_parts, sol_ref, res_ref):
    chunks = len(sol_parts)
    cw = width // chunks
    half = cw // 2
    per = LANES // width
    lower = lax.broadcasted_iota(jnp.int32, (half, LANES), 1) < HALF

    def step(g, _):
        lanes = pl.ds(pl.multiple_of(g * LANES, LANES), LANES)
        for out_ref, parts in ((sol_ref, sol_parts), (res_ref, res_parts)):
            rows = [part[g * per + z, :cw, :] for z in range(per) for part in parts]
            out_ref[:LANES, lanes] = jnp.concatenate(rows, 0).T
        rows = []
        for z in range(per):
            for sol, res in zip(sol_parts, res_parts):
                a = sol[g * per + z, cw:, :]
                b = res[g * per + z, cw:, :]
                rows.append(jnp.where(lower, a, pltpu.roll(b, HALF, 1)))
                rows.append(jnp.where(lower, pltpu.roll(a, HALF, 1), b))
        both = jnp.concatenate(rows, 0).T
        sol_ref[LANES:, lanes] = both[:HALF]
        res_ref[LANES:, lanes] = both[HALF:]
        return 0

    lax.fori_loop(0, sol_ref.shape[1] // LANES, step, 0)


UNROLL = 4


def fill(ext_ref, pieces, points):
    def step(i, _):
        for slot in range(ext_ref.shape[0] // points):
            here = pl.ds(slot * points + i * UNROLL, UNROLL)
            ext_ref[here] = jnp.zeros((UNROLL, *ext_ref.shape[1:]), jnp.float32)
        return 0

    lax.fori_loop(0, points // UNROLL, step, 0)

    def copy(i, _):
        for ref, slot in pieces:
            ext_ref[pl.ds(slot * points + i * UNROLL, UNROLL)] = ref[pl.ds(i * UNROLL, UNROLL)]
        return 0

    lax.fori_loop(0, points // UNROLL, copy, 0)


def scaled(w_ref, row, value, cw):
    top = w_ref[0, pl.ds(row, 1), :] * value[:cw]
    low = w_ref[1, pl.ds(row, 1), :] * value[cw:]
    return top, low


def near_kernel(bands, off_ref, sign_ref, x_ref, far_ref, w_ref, theirs_ref, partial_ref, sum_ref, ext_ref):
    points, rows, _ = x_ref.shape
    cw = rows * 2 // 3
    sign = sign_ref[0]
    own = jnp.where(sign > 0, REACH, REACH + 1)
    fill(ext_ref, [(x_ref, own), (far_ref, own + 2 * sign)], points)

    for out_ref, weights, shift in ((partial_ref, theirs_ref, sign), (sum_ref, w_ref, 0)):
        starts = [(own + shift) * points + off_ref[b] for b in range(bands)]

        def step(i, _):
            for u in range(UNROLL):
                p = i * UNROLL + u
                if out_ref is sum_ref:
                    top, low = scaled(weights, bands * points + p, x_ref[p], cw)
                else:
                    top, low = None, None
                for b in range(bands):
                    t, l = scaled(weights, b * points + p, ext_ref[starts[b] + p], cw)
                    top, low = (t, l) if top is None else (top + t, low + l)
                out_ref[p, :cw, :] = top
                out_ref[p, cw:, :] = low
            return 0

        lax.fori_loop(0, points // UNROLL, step, 0)


def near(offsets, sign, x, first, w, theirs):
    bands = offsets.shape[0]
    points, rows, _ = x.shape
    out = jax.ShapeDtypeStruct(x.shape, x.dtype)
    return pl.pallas_call(
        functools.partial(near_kernel, bands),
        out_shape=(out, out),
        in_specs=[SMEM, SMEM, VMEM, VMEM, VMEM, VMEM],
        out_specs=(VMEM, VMEM),
        scratch_shapes=[pltpu.VMEM(((2 * REACH + 2) * points, rows, LANES), jnp.float32)],
        compiler_params=params(),
        cost_estimate=pl.CostEstimate(flops=1000000000, bytes_accessed=6 * x.size * 4, transcendentals=0),
        name="near",
    )(offsets, sign, x, first, w, theirs)


def halves(value):
    high = value.astype(jnp.bfloat16)
    low = (value - high.astype(jnp.float32)).astype(jnp.bfloat16)
    return high, low


def product(high, low, w_high, w_low):
    dot = functools.partial(jnp.dot, preferred_element_type=jnp.float32)
    return dot(high, w_high) + (dot(low, w_high) + dot(high, w_low))


def stage(high_ref, low_ref, at, ref, cw):
    points = ref.shape[0]
    half = cw // 2
    count = points * half
    low = ref[:, cw:, :].reshape(count, LANES)
    turned = pltpu.roll(low, HALF, 1)
    for part, top, rest in ((0, ref[:, :half, :], low), (1, ref[:, half:cw, :], turned)):
        rows = slice(part * count, (part + 1) * count)
        for n, value in enumerate((top.reshape(count, LANES), rest)):
            columns = slice(at + n * LANES, at + (n + 1) * LANES)
            high, small = halves(value)
            high_ref[rows, columns] = high
            low_ref[rows, columns] = small


def unstage(value, points, cw):
    half = cw // 2
    count = points * half
    first, second = value[:count], value[count:]
    top = [v[:, :LANES].reshape(points, half, LANES) for v in (first, second)]
    low = first[:, LANES:] + pltpu.roll(second[:, LANES:], HALF, 1)
    return top, low.reshape(points, half, LANES)


def wall_kernel(n_blocks, f_ref, mh_ref, ml_ref, *rest):
    blocks = rest[:n_blocks]
    out_ref, high_ref, low_ref = rest[n_blocks:]
    points, rows, _ = f_ref.shape
    cw = rows * 2 // 3
    half = cw // 2
    for k, ref in enumerate(blocks):
        stage(high_ref, low_ref, 2 * LANES * k, ref, cw)
    result = product(high_ref[...], low_ref[...], mh_ref[...], ml_ref[...])
    top, low = unstage(result, points, cw)
    out_ref[:, :half, :] = f_ref[:, :half, :] - top[0]
    out_ref[:, half:cw, :] = f_ref[:, half:cw, :] - top[1]
    out_ref[:, cw:, :] = f_ref[:, cw:, :] - low


def wall(f, mh, ml, blocks):
    points, rows, _ = f.shape
    n_blocks = len(blocks)
    m_rows = points * rows * 2 // 3
    return pl.pallas_call(
        functools.partial(wall_kernel, n_blocks),
        out_shape=jax.ShapeDtypeStruct(f.shape, f.dtype),
        in_specs=[VMEM] * (3 + n_blocks),
        out_specs=VMEM,
        scratch_shapes=[pltpu.VMEM((m_rows, 2 * LANES * n_blocks), jnp.bfloat16)] * 2,
        compiler_params=params(),
        cost_estimate=pl.CostEstimate(flops=3000000000, bytes_accessed=8 * f.size * 4, transcendentals=0),
        name="wall",
    )(f, mh, ml, *blocks)


def last_kernel(bands, width, n_earlier, off_ref, sign_ref, g_ref, s_ref, t_ref, x_ref, far_ref, w_ref, bh_ref, bl_ref, *rest):
    earlier = rest[: 2 * n_earlier]
    rest = rest[2 * n_earlier :]
    if width:
        sol_ref, res_ref, ext_ref, high_ref, low_ref, x_new_ref, r_ref = rest
    else:
        x_new_ref, r_ref, ext_ref, high_ref, low_ref = rest
    points, rows, _ = x_ref.shape
    cw = rows * 2 // 3
    half = cw // 2
    sign = sign_ref[0]
    fill(ext_ref, [(far_ref, 1)], points)

    def begin(i, _):
        here = pl.ds(i * UNROLL, UNROLL)
        r_ref[here] = g_ref[here] - s_ref[here] - t_ref[here]
        return 0

    lax.fori_loop(0, points // UNROLL, begin, 0)
    for b in range(bands):
        start = off_ref[b] + 2 * sign * points

        @pl.when(jnp.logical_and(start > -points, start < points))
        def _():
            def step(i, _):
                for u in range(UNROLL):
                    p = i * UNROLL + u
                    top, low = scaled(w_ref, b * points + p, ext_ref[points + start + p], cw)
                    r_ref[p, :cw, :] = r_ref[p, :cw, :] - top
                    r_ref[p, cw:, :] = r_ref[p, cw:, :] - low
                return 0

            lax.fori_loop(0, points // UNROLL, step, 0)

    stage(high_ref, low_ref, 0, r_ref, cw)
    result = product(high_ref[...], low_ref[...], bh_ref[...], bl_ref[...])
    top, low = unstage(result, points, cw)
    x_new_ref[:, :half, :] = x_ref[:, :half, :] + top[0]
    x_new_ref[:, half:cw, :] = x_ref[:, half:cw, :] + top[1]
    x_new_ref[:, cw:, :] = x_ref[:, cw:, :] + low
    if width:
        join(width, [*earlier[::2], x_new_ref], [*earlier[1::2], r_ref], sol_ref, res_ref)


def last(offsets, sign, g, s, t, x, second, w, bh, bl, earlier, width):
    bands = offsets.shape[0]
    points, rows, _ = x.shape
    chunk = pltpu.VMEM(x.shape, jnp.float32)
    if width:
        out = jax.ShapeDtypeStruct((LANES + HALF, points * width), x.dtype)
    else:
        out = jax.ShapeDtypeStruct(x.shape, x.dtype)
    m_rows = points * rows * 2 // 3
    return pl.pallas_call(
        functools.partial(last_kernel, bands, width, len(earlier) // 2),
        out_shape=(out, out),
        in_specs=[SMEM, SMEM] + [VMEM] * (8 + len(earlier)),
        out_specs=(VMEM, VMEM),
        scratch_shapes=[
            pltpu.VMEM((3 * points, rows, LANES), jnp.float32),
            pltpu.VMEM((m_rows, 2 * LANES), jnp.bfloat16),
            pltpu.VMEM((m_rows, 2 * LANES), jnp.bfloat16),
        ]
        + ([chunk, chunk] if width else []),
        compiler_params=params(),
        cost_estimate=pl.CostEstimate(flops=1000000000, bytes_accessed=8 * x.size * 4, transcendentals=0),
        name="last",
    )(offsets, sign, g, s, t, x, second, w, bh, bl, *earlier)


def two_parts(value):
    high = lax.reduce_precision(value, 8, 7)
    return high.astype(jnp.bfloat16), (value - high).astype(jnp.bfloat16)


def right_side(matrix):
    rows = matrix.shape[0]
    return jnp.pad(matrix.T, ((0, 2 * LANES - rows), (0, 2 * LANES - rows)))


def wall_rows(wall_even, wall_odd, rows):
    count = lax.axis_size("wall")
    index = lax.axis_index("wall")
    upper = index < count // 2
    at = jnp.where(upper, index, count - 1 - index) * rows
    even = lax.dynamic_slice_in_dim(wall_even, at, rows, 0)
    odd = lax.dynamic_slice_in_dim(wall_odd, at, rows, 0)
    same = 0.5 * (even + odd)
    cross = 0.5 * (even - odd)
    full = jnp.concatenate([same, jnp.flip(cross, 1)], 1)
    full = jnp.where(upper, full, jnp.flip(full, (0, 1)))
    blocks = jnp.stack([right_side(full[:, k * rows : (k + 1) * rows]) for k in range(count)])
    ordered = jnp.concatenate([lax.dynamic_index_in_dim(blocks, index ^ k, 0, False) for k in range(count)], 0)
    return two_parts(ordered)


def after(value, *others):
    return lax.optimization_barrier((value, *others))[0]


def sweeps(forcing, start, wall_even, wall_odd, diag_shift, band_coef, offsets, pattern, block_inv):
    rows, breadth = start.shape
    points = diag_shift.shape[1]
    bands = band_coef.shape[0]
    width = breadth // points
    chunks = CHUNKS
    n_wall = lax.axis_size("wall")
    sign = jnp.where(lax.axis_index("span") % 2 == 0, 1, -1).astype(jnp.int32)[None]

    raw_first = far(start, True)
    state = list(split(start, chunks, points))
    weights = jnp.swapaxes(band_coef, 1, 2) * pattern.astype(jnp.float32)[:, :, None]
    weights = jnp.concatenate([weights, diag_shift.T[None]], 0).reshape((bands + 1) * points, rows)
    low = weights[:, LANES:]
    own_w = jnp.stack([weights[:, :LANES], jnp.concatenate([low, low], 1)])
    their_w = partner(own_w[:, : bands * points])
    mh, ml = wall_rows(wall_even, wall_odd, rows)
    bh, bl = two_parts(right_side(block_inv))
    f = split(forcing, chunks, points)
    residual = [None] * chunks
    arrived = raw_first
    order = [0]
    bit = n_wall // 2
    while bit:
        order = order + [o ^ bit for o in order]
        bit //= 2
    for sweep in range(SWEEPS):
        final_sweep = sweep == SWEEPS - 1
        if sweep:
            firsts = [far(after(state[k], arrived), True) for k in range(chunks)]
            arrived = firsts[-1]
        else:
            firsts = split(raw_first, chunks, points)
        seconds = [far(after(state[k], arrived), False) for k in range(chunks)]
        arrived = seconds[-1]
        walls = []
        for k in range(chunks):
            got = [state[k]]
            bit = n_wall // 2
            while bit:
                got = got + [exchange(v, bit) for v in got]
                bit //= 2
            walls.append([got[order.index(o)] for o in range(n_wall)])
        theirs = []
        sums = []
        for k in range(chunks):
            partial, own_sum = near(offsets, sign, state[k], firsts[k], own_w, their_w)
            sums.append(own_sum)
            theirs.append(partner(partial))
        new = []
        for k in range(chunks):
            g = wall(f[k], mh, ml, walls[k])
            final = final_sweep and k == chunks - 1
            earlier = [a for pair in new for a in pair] if final else []
            new.append(
                last(
                    offsets,
                    sign,
                    g,
                    sums[k],
                    theirs[k],
                    state[k],
                    seconds[k],
                    own_w,
                    bh,
                    bl,
                    earlier,
                    width if final else 0,
                )
            )
        state = [pair[0] for pair in new]
        residual = [pair[1] for pair in new]
    return state[-1], residual[-1]


def solution(mesh):
    in_specs = (
        P("wall", "span"),
        P("wall", "span"),
        P(),
        P(),
        P("wall", "span"),
        P(None, "wall", "span"),
        P(),
        P(None, "span"),
        P("wall", None),
    )
    out_specs = (P("wall", "span"), P("wall", "span"))
    return jax.shard_map(sweeps, mesh=mesh, in_specs=in_specs, out_specs=out_specs, check_vma=False)
```

profile of v0, /device:TPU:20, one launch (start us, length us, event | category | flops | bytes accessed | tf_op | source)
XLA Modules:
  0.0 196.0 jit_solution(4209450873650384739)
XLA Ops:
  0.6 5.0 %split.4 = (f32[64,24,128]{2,1,0:T(8,128)}, f32[64,24,128]{2,1,0:T(8,128)}) custom-call(f32[192,2048]{1,0:T(8,128)} %x_ref.3), custom_call_target="tpu_custom_call" | custom-call | bytes 3145728 | tf_op jit(solution)/shard_map/split/pallas_call | solution.py:71
  6.5 1.5 collective-permute-start.1
  8.1 1.1 add_multiply_fusion
  9.2 0.9 reverse.3
  10.1 2.0 %multiply_bitcast_fusion = f32[8,64,192]{2,1,0:T(8,128)} fusion(f32[8,192,64]{1,2,0:T(8,128)} %param.14, f32[8,64]{1,0:T(8,128)S(1)} %convert_element_type.23), kind=kLoop, calls=%fused_computation.11 | loop fusion | flops 98304 | bytes 788480 | tf_op jit(solution)/shard_map/mul | solution.py:355
  13.0 7.1 %rev.9 = f32[192,768]{1,0:T(8,128)} reverse(f32[192,768]{1,0:T(8,128)} %pad_maximum_fusion.3), dimensions={0,1} | reverse | bytes 1179648 | tf_op jit(solution)/shard_map/jit(_flip)/rev | solution.py:334
  20.1 1.2 broadcast_select_fusion
  21.7 0.9 pad_bitcast_fusion
  22.7 1.7 copy.15
  24.4 1.9 collective-permute-done.14.rest_2_
  27.1 14.8 %collective-permute-done.1.rest_2_ = f32[64,24,128]{2,1,0:T(8,128)S(1)} collective-permute-done((f32[64,24,128]{2,1,0:T(8,128)}, f32[64,24,128]{2,1,0:T(8,128)S(1)}, u32[]{:S(2)}, u32[]{:S(2)}) %collective-permute-start.1) | collective-permute-done | bytes 786464 | tf_op jit(solution)/shard_map/ppermute | solution.py:20
  41.9 1.5 collective-permute-start.4
  43.4 1.1 pad_maximum_fusion
  44.6 1.0 constant_dynamic-slice_fusion.3
  45.6 1.9 copy.12
  47.6 1.8 copy.13
  49.4 1.8 copy.14
  51.2 1.8 copy.11
  53.0 2.4 %split.3 = (f32[64,24,128]{2,1,0:T(8,128)S(1)}, f32[64,24,128]{2,1,0:T(8,128)S(1)}) custom-call(f32[192,2048]{1,0:T(8,128)S(1)} %copy-done), custom_call_target="tpu_custom_call" | custom-call | bytes 3145728 | tf_op jit(solution)/shard_map/split/pallas_call | solution.py:71
  55.3 0.9 copy-done.4
  56.2 0.9 copy-done.6
  57.1 1.1 pad_maximum_fusion.2.w_ref
  58.2 2.4 %split.5 = (f32[64,24,128]{2,1,0:T(8,128)S(1)}, f32[64,24,128]{2,1,0:T(8,128)S(1)}) custom-call(f32[192,2048]{1,0:T(8,128)S(1)} %collective-permute-done.3.x_ref), custom_call_target="tpu_custom_call" | custom-call | bytes 3145728 | tf_op jit(solution)/shard_map/split/pallas_call | solution.py:71
  60.6 3.4 %near.4 = (f32[64,24,128]{2,1,0:T(8,128)S(1)}, f32[64,24,128]{2,1,0:T(8,128)S(1)}) custom-call(s32[8]{0:T(128)S(1)} %copy-done.1, s32[1]{0:T(128)} %bitcast.sign_ref, f32[64,24,128]{2,1,0:T(8,128)} %get-tuple-element.31.rest_0_.x_ref, f32[64,24,128]{2,1,0:T(8,128)S(1)} %get-tuple-element.28.far_ref, f32[2,576,128]{2,1,0:T(8,128)S(1)} %pad_maximum_fusion.2.w_ref, ...), custom_call_target="tpu_custom_call" | custom-call | flops 1000000000 | bytes 4718592 | tf_op jit(solution)/shard_map/near/pallas_call | solution.py:166
  64.6 1.6 collective-permute-start.6
  66.2 3.5 %near.6 = (f32[64,24,128]{2,1,0:T(8,128)S(1)}, f32[64,24,128]{2,1,0:T(8,128)S(1)}) custom-call(s32[8]{0:T(128)S(1)} %copy-done.1, s32[1]{0:T(128)} %bitcast.sign_ref, f32[64,24,128]{2,1,0:T(8,128)} %get-tuple-element.42.rest_0_.x_ref, f32[64,24,128]{2,1,0:T(8,128)S(1)} %get-tuple-element.39.far_ref, f32[2,576,128]{2,1,0:T(8,128)S(1)} %pad_maximum_fusion.2.w_ref, ...), custom_call_target="tpu_custom_call" | custom-call | flops 1000000000 | bytes 4718592 | tf_op jit(solution)/shard_map/near/pallas_call | solution.py:166
  70.1 1.6 collective-permute-start.17
  71.9 3.9 %wall.6.g_ref = f32[64,24,128]{2,1,0:T(8,128)S(1)} custom-call(f32[64,24,128]{2,1,0:T(8,128)S(1)} %copy-done.7, bf16[1024,256]{1,0:T(8,128)(2,1)S(1)} %get-tuple-element.53.mh_ref, bf16[1024,256]{1,0:T(8,128)(2,1)S(1)} %get-tuple-element.52.ml_ref, f32[64,24,128]{2,1,0:T(8,128)} %get-tuple-element.42.rest_0_.x_ref, ...), custom_call_target="tpu_custom_call" | custom-call | flops 3000000000 | bytes 6291456 | tf_op jit(solution)/shard_map/wall/pallas_call | solution.py:232
  75.8 3.5 %wall.4.g_ref = f32[64,24,128]{2,1,0:T(8,128)S(1)} custom-call(f32[64,24,128]{2,1,0:T(8,128)S(1)} %copy-done.5, bf16[1024,256]{1,0:T(8,128)(2,1)S(1)} %get-tuple-element.53.mh_ref, bf16[1024,256]{1,0:T(8,128)(2,1)S(1)} %get-tuple-element.52.ml_ref, f32[64,24,128]{2,1,0:T(8,128)} %get-tuple-element.31.rest_0_.x_ref, ...), custom_call_target="tpu_custom_call" | custom-call | flops 3000000000 | bytes 6291456 | tf_op jit(solution)/shard_map/wall/pallas_call | solution.py:232
  79.3 5.1 %collective-permute-done.5.t_ref = f32[64,24,128]{2,1,0:T(8,128)S(1)} collective-permute-done((f32[64,24,128]{2,1,0:T(8,128)S(1)}, f32[64,24,128]{2,1,0:T(8,128)S(1)}, u32[]{:S(2)}, u32[]{:S(2)}) %collective-permute-start.5) | collective-permute-done | bytes 786464 | tf_op jit(solution)/shard_map/ppermute | solution.py:25
  85.2 2.9 %last.4 = (f32[64,24,128]{2,1,0:T(8,128)S(1)}, f32[64,24,128]{2,1,0:T(8,128)}) custom-call(s32[8]{0:T(128)S(1)} %copy-done.1, s32[1]{0:T(128)} %bitcast.sign_ref, f32[64,24,128]{2,1,0:T(8,128)S(1)} %wall.4.g_ref, f32[64,24,128]{2,1,0:T(8,128)S(1)} %get-tuple-element.29.s_ref, f32[64,24,128]{2,1,0:T(8,128)S(1)} %collective-permute-done.5.t_ref, ...), custom_call_target="tpu_custom_call" | custom-call | flops 1000000000 | bytes 6291456 | tf_op jit(solution)/shard_map/last/pallas_call | solution.py:297
  88.5 12.2 %collective-permute-done.16.t_ref = f32[64,24,128]{2,1,0:T(8,128)S(1)} collective-permute-done((f32[64,24,128]{2,1,0:T(8,128)S(1)}, f32[64,24,128]{2,1,0:T(8,128)S(1)}, u32[]{:S(2)}, u32[]{:S(2)}) %collective-permute-start.16) | collective-permute-done | bytes 786464 | tf_op jit(solution)/shard_map/ppermute | solution.py:25
  100.7 25.7 %collective-permute-done.17.far_ref = f32[64,24,128]{2,1,0:T(8,128)S(1)} collective-permute-done((f32[64,24,128]{2,1,0:T(8,128)}, f32[64,24,128]{2,1,0:T(8,128)S(1)}, u32[]{:S(2)}, u32[]{:S(2)}) %collective-permute-start.17) | collective-permute-done | bytes 786464 | tf_op jit(solution)/shard_map/ppermute | solution.py:34
  126.5 2.9 %last.5 = (f32[64,24,128]{2,1,0:T(8,128)S(1)}, f32[64,24,128]{2,1,0:T(8,128)}) custom-call(s32[8]{0:T(128)S(1)} %copy-done.1, s32[1]{0:T(128)} %bitcast.sign_ref, f32[64,24,128]{2,1,0:T(8,128)S(1)} %wall.6.g_ref, f32[64,24,128]{2,1,0:T(8,128)S(1)} %get-tuple-element.40.s_ref, f32[64,24,128]{2,1,0:T(8,128)S(1)} %collective-permute-done.16.t_ref, ...), custom_call_target="tpu_custom_call" | custom-call | flops 1000000000 | bytes 6291456 | tf_op jit(solution)/shard_map/last/pallas_call | solution.py:297
  129.4 2.0 %collective-permute-start.8 = (f32[64,24,128]{2,1,0:T(8,128)S(1)}, f32[64,24,128]{2,1,0:T(8,128)S(1)}, u32[]{:S(2)}, u32[]{:S(2)}) collective-permute-start(f32[64,24,128]{2,1,0:T(8,128)S(1)} %get-tuple-element.36.rest_0_.x_ref), channel_id=1, source_target_pairs={{0,2},{1,3},{2,0},{3,1},{4,6},{5,7},{6,4},{7,5},{8,10},{9,11},{10,... | collective-permute-start | bytes 2359304 | tf_op jit(solution)/shard_map/ppermute | solution.py:20
  131.4 2.0 %collective-permute-start.23 = (f32[64,24,128]{2,1,0:T(8,128)S(1)}, f32[64,24,128]{2,1,0:T(8,128)S(1)}, u32[]{:S(2)}, u32[]{:S(2)}) collective-permute-start(f32[64,24,128]{2,1,0:T(8,128)S(1)} %get-tuple-element.47.rest_0_.x_ref), channel_id=1, source_target_pairs={{0,8},{4,28},{8,16},{12,4},{16,24},{20,12},{24,0},{28,20},{1,9},{5... | collective-permute-start | bytes 2359304 | tf_op jit(solution)/shard_map/ppermute | solution.py:34
  133.4 16.2 %collective-permute-done.19.rest_2_ = f32[64,24,128]{2,1,0:T(8,128)S(1)} collective-permute-done((f32[64,24,128]{2,1,0:T(8,128)S(1)}, f32[64,24,128]{2,1,0:T(8,128)S(1)}, u32[]{:S(2)}, u32[]{:S(2)}) %collective-permute-start.19) | collective-permute-done | bytes 786464 | tf_op jit(solution)/shard_map/ppermute | solution.py:20
  149.6 3.1 %near.7 = (f32[64,24,128]{2,1,0:T(8,128)S(1)}, f32[64,24,128]{2,1,0:T(8,128)S(1)}) custom-call(s32[8]{0:T(128)S(1)} %copy-done.1, s32[1]{0:T(128)} %bitcast.sign_ref, f32[64,24,128]{2,1,0:T(8,128)S(1)} %get-tuple-element.47.rest_0_.x_ref, f32[64,24,128]{2,1,0:T(8,128)S(1)} %collective-permute-done.21.far_ref, f32[2,576,128]{2,1,0:T(8,128)S(1)} %pad_maximum_fusion.2.w_ref, ...), custom_call_target="tpu_custom_call" | custom-call | flops 1000000000 | bytes 4718592 | tf_op jit(solution)/shard_map/near/pallas_call | solution.py:166
  153.4 4.7 %collective-permute-done.8.rest_2_ = f32[64,24,128]{2,1,0:T(8,128)S(1)} collective-permute-done((f32[64,24,128]{2,1,0:T(8,128)S(1)}, f32[64,24,128]{2,1,0:T(8,128)S(1)}, u32[]{:S(2)}, u32[]{:S(2)}) %collective-permute-start.8) | collective-permute-done | bytes 786464 | tf_op jit(solution)/shard_map/ppermute | solution.py:20
  158.0 3.1 %near.5 = (f32[64,24,128]{2,1,0:T(8,128)S(1)}, f32[64,24,128]{2,1,0:T(8,128)S(1)}) custom-call(s32[8]{0:T(128)S(1)} %copy-done.1, s32[1]{0:T(128)} %bitcast.sign_ref, f32[64,24,128]{2,1,0:T(8,128)S(1)} %get-tuple-element.36.rest_0_.x_ref, f32[64,24,128]{2,1,0:T(8,128)S(1)} %collective-permute-done.10.far_ref, f32[2,576,128]{2,1,0:T(8,128)S(1)} %pad_maximum_fusion.2.w_ref, ...), custom_call_target="tpu_custom_call" | custom-call | flops 1000000000 | bytes 4718592 | tf_op jit(solution)/shard_map/near/pallas_call | solution.py:166
  161.2 1.8 collective-permute-start.12
  163.0 1.9 wall.7.g_ref
  164.9 8.3 %collective-permute-done.22.t_ref = f32[64,24,128]{2,1,0:T(8,128)S(1)} collective-permute-done((f32[64,24,128]{2,1,0:T(8,128)S(1)}, f32[64,24,128]{2,1,0:T(8,128)S(1)}, u32[]{:S(2)}, u32[]{:S(2)}) %collective-permute-start.22) | collective-permute-done | bytes 786464 | tf_op jit(solution)/shard_map/ppermute | solution.py:25
  173.2 2.2 %last.6 = (f32[64,24,128]{2,1,0:T(8,128)S(1)}, f32[64,24,128]{2,1,0:T(8,128)S(1)}) custom-call(s32[8]{0:T(128)S(1)} %copy-done.1, s32[1]{0:T(128)} %bitcast.sign_ref, f32[64,24,128]{2,1,0:T(8,128)S(1)} %wall.7.g_ref, f32[64,24,128]{2,1,0:T(8,128)S(1)} %get-tuple-element.45.s_ref, f32[64,24,128]{2,1,0:T(8,128)S(1)} %collective-permute-done.22.t_ref, ...), custom_call_target="tpu_custom_call" | custom-call | flops 1000000000 | bytes 6291456 | tf_op jit(solution)/shard_map/last/pallas_call | solution.py:297
  175.5 1.9 wall.5.g_ref
  177.4 3.8 %collective-permute-done.12.far_ref = f32[64,24,128]{2,1,0:T(8,128)S(1)} collective-permute-done((f32[64,24,128]{2,1,0:T(8,128)S(1)}, f32[64,24,128]{2,1,0:T(8,128)S(1)}, u32[]{:S(2)}, u32[]{:S(2)}) %collective-permute-start.12) | collective-permute-done | bytes 786464 | tf_op jit(solution)/shard_map/ppermute | solution.py:34
  181.2 8.4 %collective-permute-done.11.t_ref = f32[64,24,128]{2,1,0:T(8,128)S(1)} collective-permute-done((f32[64,24,128]{2,1,0:T(8,128)S(1)}, f32[64,24,128]{2,1,0:T(8,128)S(1)}, u32[]{:S(2)}, u32[]{:S(2)}) %collective-permute-start.11) | collective-permute-done | bytes 786464 | tf_op jit(solution)/shard_map/ppermute | solution.py:25
  189.6 6.4 %last.7 = (f32[192,2048]{1,0:T(8,128)}, f32[192,2048]{1,0:T(8,128)}) custom-call(s32[8]{0:T(128)S(1)} %copy-done.1, s32[1]{0:T(128)} %bitcast.sign_ref, f32[64,24,128]{2,1,0:T(8,128)S(1)} %wall.5.g_ref, f32[64,24,128]{2,1,0:T(8,128)S(1)} %get-tuple-element.34.s_ref, f32[64,24,128]{2,1,0:T(8,128)S(1)} %collective-permute-done.11.t_ref, ...), custom_call_target="tpu_custom_call" | custom-call | flops 1000000000 | bytes 6291456 | tf_op jit(solution)/shard_map/last/pallas_call | solution.py:297
  (76 shorter events, 6.3 us)
Async XLA Ops:
  5.6 4.5 %copy-start.17 = (s32[8,64]{1,0:T(8,128)S(1)}, s32[8,64]{1,0:T(8,128)}, u32[]{:S(2)}) copy-start(s32[8,64]{1,0:T(8,128)} %param.16) | copy-start | bytes 6148
  5.6 20.7 %collective-permute-start.14 = (f32[64,24,128]{2,1,0:T(8,128)}, f32[64,24,128]{2,1,0:T(8,128)}, u32[]{:S(2)}, u32[]{:S(2)}) collective-permute-start(f32[64,24,128]{2,1,0:T(8,128)} %get-tuple-element.42.rest_0_.x_ref), channel_id=1, source_target_pairs={{0,2},{1,3},{2,0},{3,1},{4,6},{5,7},{6,4},{7,5},{8,10},{9,11},{10,... | collective-permute-start | bytes 2359304 | tf_op jit(solution)/shard_map/ppermute | solution.py:20
  6.1 58.5 %collective-permute-start.13 = (f32[64,24,128]{2,1,0:T(8,128)}, f32[64,24,128]{2,1,0:T(8,128)}, u32[]{:S(2)}, u32[]{:S(2)}) collective-permute-start(f32[64,24,128]{2,1,0:T(8,128)} %get-tuple-element.42.rest_0_.x_ref), channel_id=1, source_target_pairs={{0,1},{1,0},{2,3},{3,2},{4,5},{5,4},{6,7},{7,6},{8,9},{9,8},{10,11... | collective-permute-start | bytes 2359304 | tf_op jit(solution)/shard_map/ppermute | solution.py:20
  6.1 39.5 %collective-permute-start.3 = (f32[192,2048]{1,0:T(8,128)}, f32[192,2048]{1,0:T(8,128)S(1)}, u32[]{:S(2)}, u32[]{:S(2)}) collective-permute-start(f32[192,2048]{1,0:T(8,128)} %x_ref.3), channel_id=1, source_target_pairs={{0,24},{4,12},{8,0},{12,20},{16,8},{20,28},{24,16},{28,4},{1,25},{... | collective-permute-start | bytes 4718600 | tf_op jit(solution)/shard_map/ppermute | solution.py:34
  6.5 35.4 %collective-permute-start.1 = (f32[64,24,128]{2,1,0:T(8,128)}, f32[64,24,128]{2,1,0:T(8,128)S(1)}, u32[]{:S(2)}, u32[]{:S(2)}) collective-permute-start(f32[64,24,128]{2,1,0:T(8,128)} %get-tuple-element.31.rest_0_.x_ref), channel_id=1, source_target_pairs={{0,2},{1,3},{2,0},{3,1},{4,6},{5,7},{6,4},{7,5},{8,10},{9,11},{10,... | collective-permute-start | bytes 2359304 | tf_op jit(solution)/shard_map/ppermute | solution.py:20
  8.1 61.6 %collective-permute-start = (f32[64,24,128]{2,1,0:T(8,128)}, f32[64,24,128]{2,1,0:T(8,128)}, u32[]{:S(2)}, u32[]{:S(2)}) collective-permute-start(f32[64,24,128]{2,1,0:T(8,128)} %get-tuple-element.31.rest_0_.x_ref), channel_id=1, source_target_pairs={{0,1},{1,0},{2,3},{3,2},{4,5},{5,4},{6,7},{7,6},{8,9},{9,8},{10,11... | collective-permute-start | bytes 2359304 | tf_op jit(solution)/shard_map/ppermute | solution.py:20
  13.0 8.3 %copy-start.16 = (f32[192,64]{0,1:T(8,128)S(1)}, f32[192,64]{0,1:T(8,128)}, u32[]{:S(2)}) copy-start(f32[192,64]{0,1:T(8,128)} %param.13) | copy-start | bytes 147460
  20.1 1.2 copy-start.10
  21.7 22.8 %copy-start.8 = (f32[1,576,128]{2,1,0:T(8,128)}, f32[1,576,128]{2,1,0:T(8,128)S(1)}, u32[]{:S(2)}) copy-start(f32[1,576,128]{2,1,0:T(8,128)S(1)} %get-tuple-element.68) | copy-start | bytes 884740
  21.7 22.8 %copy-start.9 = (f32[1,576,128]{2,1,0:T(8,128)}, f32[1,576,128]{2,1,0:T(8,128)S(1)}, u32[]{:S(2)}) copy-start(f32[1,576,128]{2,1,0:T(8,128)S(1)} %get-tuple-element.69) | copy-start | bytes 884740
  26.3 43.8 %collective-permute-start.15 = (f32[64,24,128]{2,1,0:T(8,128)}, f32[64,24,128]{2,1,0:T(8,128)}, u32[]{:S(2)}, u32[]{:S(2)}) collective-permute-start(f32[64,24,128]{2,1,0:T(8,128)} %collective-permute-done.14.rest_2_), channel_id=1, source_target_pairs={{0,1},{1,0},{2,3},{3,2},{4,5},{5,4},{6,7},{7,6},{8,9},{9,8},{10,11... | collective-permute-start | bytes 2359304 | tf_op jit(solution)/shard_map/ppermute | solution.py:20
  41.9 2.6 %copy-start.2 = (f32[64,24,128]{2,1,0:T(8,128)}, f32[64,24,128]{2,1,0:T(8,128)S(1)}, u32[]{:S(2)}) copy-start(f32[64,24,128]{2,1,0:T(8,128)S(1)} %collective-permute-done.1.rest_2_) | copy-start | bytes 2359300
  41.9 18.7 %collective-permute-start.4 = (f32[2,512,128]{2,1,0:T(8,128)}, f32[2,512,128]{2,1,0:T(8,128)}, u32[]{:S(2)}, u32[]{:S(2)}) collective-permute-start(f32[2,512,128]{2,1,0:T(8,128)} %fusion.1), channel_id=1, source_target_pairs={{0,4},{4,0},{8,12},{12,8},{16,20},{20,16},{24,28},{28,24},{1,5},{5... | collective-permute-start | bytes 1572872 | tf_op jit(solution)/shard_map/ppermute | solution.py:25
  44.6 1.0 copy-start.15
  45.6 7.4 %copy-start = (f32[192,2048]{1,0:T(8,128)S(1)}, f32[192,2048]{1,0:T(8,128)}, u32[]{:S(2)}) copy-start(f32[192,2048]{1,0:T(8,128)} %x_ref.2) | copy-start | bytes 4718596
  45.6 30.2 %collective-permute-start.2 = (f32[64,24,128]{2,1,0:T(8,128)}, f32[64,24,128]{2,1,0:T(8,128)}, u32[]{:S(2)}, u32[]{:S(2)}) collective-permute-start(f32[64,24,128]{2,1,0:T(8,128)} %copy-done.2), channel_id=1, source_target_pairs={{0,1},{1,0},{2,3},{3,2},{4,5},{5,4},{6,7},{7,6},{8,9},{9,8},{10,11... | collective-permute-start | bytes 2359304 | tf_op jit(solution)/shard_map/ppermute | solution.py:20
  55.3 0.9 copy-start.4
  56.2 0.9 copy-start.6
  57.1 3.5 %copy-start.1 = (s32[8]{0:T(128)S(1)}, s32[8]{0:T(128)}, u32[]{:S(2)}) copy-start(s32[8]{0:T(128)} %off_ref.15) | copy-start | bytes 100
  64.0 20.5 %collective-permute-start.5 = (f32[64,24,128]{2,1,0:T(8,128)S(1)}, f32[64,24,128]{2,1,0:T(8,128)S(1)}, u32[]{:S(2)}, u32[]{:S(2)}) collective-permute-start(f32[64,24,128]{2,1,0:T(8,128)S(1)} %get-tuple-element.30), channel_id=1, source_target_pairs={{0,4},{4,0},{8,12},{12,8},{16,20},{20,16},{24,28},{28,24},{1,5},{5... | collective-permute-start | bytes 2359304 | tf_op jit(solution)/shard_map/ppermute | solution.py:25
  64.6 20.6 %collective-permute-start.6 = (f32[64,24,128]{2,1,0:T(8,128)}, f32[64,24,128]{2,1,0:T(8,128)S(1)}, u32[]{:S(2)}, u32[]{:S(2)}) collective-permute-start(f32[64,24,128]{2,1,0:T(8,128)} %get-tuple-element.31.rest_0_.x_ref), channel_id=1, source_target_pairs={{0,8},{4,28},{8,16},{12,4},{16,24},{20,12},{24,0},{28,20},{1,9},{5... | collective-permute-start | bytes 2359304 | tf_op jit(solution)/shard_map/ppermute | solution.py:34
  66.2 5.5 %copy-start.11 = (f32[1,256,256]{2,1,0:T(8,128)S(1)}, f32[1,256,256]{2,1,0:T(8,128)}, u32[]{:S(2)}) copy-start(f32[1,256,256]{2,1,0:T(8,128)} %copy.12) | copy-start | bytes 786436
  66.2 5.5 %copy-start.12 = (f32[1,256,256]{2,1,0:T(8,128)S(1)}, f32[1,256,256]{2,1,0:T(8,128)}, u32[]{:S(2)}) copy-start(f32[1,256,256]{2,1,0:T(8,128)} %copy.13) | copy-start | bytes 786436
  66.2 5.5 %copy-start.13 = (f32[1,256,256]{2,1,0:T(8,128)S(1)}, f32[1,256,256]{2,1,0:T(8,128)}, u32[]{:S(2)}) copy-start(f32[1,256,256]{2,1,0:T(8,128)} %copy.14) | copy-start | bytes 786436
  66.2 5.5 %copy-start.14 = (f32[1,256,256]{2,1,0:T(8,128)S(1)}, f32[1,256,256]{2,1,0:T(8,128)}, u32[]{:S(2)}) copy-start(f32[1,256,256]{2,1,0:T(8,128)} %copy.11) | copy-start | bytes 786436
  69.6 2.2 %copy-start.7 = (f32[64,24,128]{2,1,0:T(8,128)S(1)}, f32[64,24,128]{2,1,0:T(8,128)}, u32[]{:S(2)}) copy-start(f32[64,24,128]{2,1,0:T(8,128)} %copy-done.6) | copy-start | bytes 2359300
  69.7 31.1 %collective-permute-start.16 = (f32[64,24,128]{2,1,0:T(8,128)S(1)}, f32[64,24,128]{2,1,0:T(8,128)S(1)}, u32[]{:S(2)}, u32[]{:S(2)}) collective-permute-start(f32[64,24,128]{2,1,0:T(8,128)S(1)} %get-tuple-element.41), channel_id=1, source_target_pairs={{0,4},{4,0},{8,12},{12,8},{16,20},{20,16},{24,28},{28,24},{1,5},{5... | collective-permute-start | bytes 2359304 | tf_op jit(solution)/shard_map/ppermute | solution.py:25
  70.1 56.4 %collective-permute-start.17 = (f32[64,24,128]{2,1,0:T(8,128)}, f32[64,24,128]{2,1,0:T(8,128)S(1)}, u32[]{:S(2)}, u32[]{:S(2)}) collective-permute-start(f32[64,24,128]{2,1,0:T(8,128)} %get-tuple-element.42.rest_0_.x_ref), channel_id=1, source_target_pairs={{0,8},{4,28},{8,16},{12,4},{16,24},{20,12},{24,0},{28,20},{1,9},{5... | collective-permute-start | bytes 2359304 | tf_op jit(solution)/shard_map/ppermute | solution.py:34
  71.9 3.9 %copy-start.3 = (f32[64,24,128]{2,1,0:T(8,128)S(1)}, f32[64,24,128]{2,1,0:T(8,128)}, u32[]{:S(2)}) copy-start(f32[64,24,128]{2,1,0:T(8,128)} %copy-done.2) | copy-start | bytes 2359300
  71.9 3.9 %copy-start.5 = (f32[64,24,128]{2,1,0:T(8,128)S(1)}, f32[64,24,128]{2,1,0:T(8,128)}, u32[]{:S(2)}) copy-start(f32[64,24,128]{2,1,0:T(8,128)} %copy-done.4) | copy-start | bytes 2359300
  88.1 43.3 %collective-permute-start.10 = (f32[64,24,128]{2,1,0:T(8,128)S(1)}, f32[64,24,128]{2,1,0:T(8,128)S(1)}, u32[]{:S(2)}, u32[]{:S(2)}) collective-permute-start(f32[64,24,128]{2,1,0:T(8,128)S(1)} %get-tuple-element.36.rest_0_.x_ref), channel_id=1, source_target_pairs={{0,24},{4,12},{8,0},{12,20},{16,8},{20,28},{24,16},{28,4},{1,25},{... | collective-permute-start | bytes 2359304 | tf_op jit(solution)/shard_map/ppermute | solution.py:34
  129.4 20.2 %collective-permute-start.19 = (f32[64,24,128]{2,1,0:T(8,128)S(1)}, f32[64,24,128]{2,1,0:T(8,128)S(1)}, u32[]{:S(2)}, u32[]{:S(2)}) collective-permute-start(f32[64,24,128]{2,1,0:T(8,128)S(1)} %get-tuple-element.47.rest_0_.x_ref), channel_id=1, source_target_pairs={{0,2},{1,3},{2,0},{3,1},{4,6},{5,7},{6,4},{7,5},{8,10},{9,11},{10,... | collective-permute-start | bytes 2359304 | tf_op jit(solution)/shard_map/ppermute | solution.py:20
  129.4 20.2 %collective-permute-start.21 = (f32[64,24,128]{2,1,0:T(8,128)S(1)}, f32[64,24,128]{2,1,0:T(8,128)S(1)}, u32[]{:S(2)}, u32[]{:S(2)}) collective-permute-start(f32[64,24,128]{2,1,0:T(8,128)S(1)} %get-tuple-element.47.rest_0_.x_ref), channel_id=1, source_target_pairs={{0,24},{4,12},{8,0},{12,20},{16,8},{20,28},{24,16},{28,4},{1,25},{... | collective-permute-start | bytes 2359304 | tf_op jit(solution)/shard_map/ppermute | solution.py:34
  129.4 23.4 %collective-permute-start.18 = (f32[64,24,128]{2,1,0:T(8,128)S(1)}, f32[64,24,128]{2,1,0:T(8,128)S(1)}, u32[]{:S(2)}, u32[]{:S(2)}) collective-permute-start(f32[64,24,128]{2,1,0:T(8,128)S(1)} %get-tuple-element.47.rest_0_.x_ref), channel_id=1, source_target_pairs={{0,1},{1,0},{2,3},{3,2},{4,5},{5,4},{6,7},{7,6},{8,9},{9,8},{10,11... | collective-permute-start | bytes 2359304 | tf_op jit(solution)/shard_map/ppermute | solution.py:20
  129.4 28.6 %collective-permute-start.8 = (f32[64,24,128]{2,1,0:T(8,128)S(1)}, f32[64,24,128]{2,1,0:T(8,128)S(1)}, u32[]{:S(2)}, u32[]{:S(2)}) collective-permute-start(f32[64,24,128]{2,1,0:T(8,128)S(1)} %get-tuple-element.36.rest_0_.x_ref), channel_id=1, source_target_pairs={{0,2},{1,3},{2,0},{3,1},{4,6},{5,7},{6,4},{7,5},{8,10},{9,11},{10,... | collective-permute-start | bytes 2359304 | tf_op jit(solution)/shard_map/ppermute | solution.py:20
  131.4 29.7 %collective-permute-start.23 = (f32[64,24,128]{2,1,0:T(8,128)S(1)}, f32[64,24,128]{2,1,0:T(8,128)S(1)}, u32[]{:S(2)}, u32[]{:S(2)}) collective-permute-start(f32[64,24,128]{2,1,0:T(8,128)S(1)} %get-tuple-element.47.rest_0_.x_ref), channel_id=1, source_target_pairs={{0,8},{4,28},{8,16},{12,4},{16,24},{20,12},{24,0},{28,20},{1,9},{5... | collective-permute-start | bytes 2359304 | tf_op jit(solution)/shard_map/ppermute | solution.py:34
  149.6 13.3 %collective-permute-start.20 = (f32[64,24,128]{2,1,0:T(8,128)S(1)}, f32[64,24,128]{2,1,0:T(8,128)S(1)}, u32[]{:S(2)}, u32[]{:S(2)}) collective-permute-start(f32[64,24,128]{2,1,0:T(8,128)S(1)} %collective-permute-done.19.rest_2_), channel_id=1, source_target_pairs={{0,1},{1,0},{2,3},{3,2},{4,5},{5,4},{6,7},{7,6},{8,9},{9,8},{10,11... | collective-permute-start | bytes 2359304 | tf_op jit(solution)/shard_map/ppermute | solution.py:20
  152.7 20.5 %collective-permute-start.22 = (f32[64,24,128]{2,1,0:T(8,128)S(1)}, f32[64,24,128]{2,1,0:T(8,128)S(1)}, u32[]{:S(2)}, u32[]{:S(2)}) collective-permute-start(f32[64,24,128]{2,1,0:T(8,128)S(1)} %get-tuple-element.46), channel_id=1, source_target_pairs={{0,4},{4,0},{8,12},{12,8},{16,20},{20,16},{24,28},{28,24},{1,5},{5... | collective-permute-start | bytes 2359304 | tf_op jit(solution)/shard_map/ppermute | solution.py:25
  152.8 22.6 %collective-permute-start.7 = (f32[64,24,128]{2,1,0:T(8,128)S(1)}, f32[64,24,128]{2,1,0:T(8,128)S(1)}, u32[]{:S(2)}, u32[]{:S(2)}) collective-permute-start(f32[64,24,128]{2,1,0:T(8,128)S(1)} %get-tuple-element.36.rest_0_.x_ref), channel_id=1, source_target_pairs={{0,1},{1,0},{2,3},{3,2},{4,5},{5,4},{6,7},{7,6},{8,9},{9,8},{10,11... | collective-permute-start | bytes 2359304 | tf_op jit(solution)/shard_map/ppermute | solution.py:20
  158.0 17.4 %collective-permute-start.9 = (f32[64,24,128]{2,1,0:T(8,128)S(1)}, f32[64,24,128]{2,1,0:T(8,128)S(1)}, u32[]{:S(2)}, u32[]{:S(2)}) collective-permute-start(f32[64,24,128]{2,1,0:T(8,128)S(1)} %collective-permute-done.8.rest_2_), channel_id=1, source_target_pairs={{0,1},{1,0},{2,3},{3,2},{4,5},{5,4},{6,7},{7,6},{8,9},{9,8},{10,11... | collective-permute-start | bytes 2359304 | tf_op jit(solution)/shard_map/ppermute | solution.py:20
  161.2 20.0 %collective-permute-start.12 = (f32[64,24,128]{2,1,0:T(8,128)S(1)}, f32[64,24,128]{2,1,0:T(8,128)S(1)}, u32[]{:S(2)}, u32[]{:S(2)}) collective-permute-start(f32[64,24,128]{2,1,0:T(8,128)S(1)} %get-tuple-element.36.rest_0_.x_ref), channel_id=1, source_target_pairs={{0,8},{4,28},{8,16},{12,4},{16,24},{20,12},{24,0},{28,20},{1,9},{5... | collective-permute-start | bytes 2359304 | tf_op jit(solution)/shard_map/ppermute | solution.py:34
  163.0 26.6 %collective-permute-start.11 = (f32[64,24,128]{2,1,0:T(8,128)S(1)}, f32[64,24,128]{2,1,0:T(8,128)S(1)}, u32[]{:S(2)}, u32[]{:S(2)}) collective-permute-start(f32[64,24,128]{2,1,0:T(8,128)S(1)} %get-tuple-element.35), channel_id=1, source_target_pairs={{0,4},{4,0},{8,12},{12,8},{16,20},{20,16},{24,28},{28,24},{1,5},{5... | collective-permute-start | bytes 2359304 | tf_op jit(solution)/shard_map/ppermute | solution.py:25
where the time goes:
time: 197 us; the launch traced here: 196 us
  waiting for transfers between devices  102 us (52%)
  Pallas kernels  48.3 us (25%)
  local copies, waits for them, and re-layouts  21.1 us (11%)
  starting transfers between devices  15.1 us (8%)
  other arithmetic  8.57 us (4%)
    ppermute x12, waiting for transfers between devices, exchange(): return lax.ppermute(value, 'wall', [(i, i ^ bit) for i in range(count)])  37.5 us
    ppermute x5, waiting for transfers between devices, partner(): return lax.ppermute(value, 'span', [(i, i ^ 1) for i in range(count)])  34.1 us
    ppermute x7, waiting for transfers between devices, far(): return lax.ppermute(value, 'span', pairs)  30.3 us
    pallas_call x4, Pallas kernels, last(): pl.pallas_call(functools.partial(last_kernel, bands, width, len(earlier)...  14.4 us
    pallas_call x4, Pallas kernels, near(): pl.pallas_call(functools.partial(near_kernel, bands), out_shape=(out, out...  13 us
    pallas_call x4, Pallas kernels, wall(): pl.pallas_call(functools.partial(wall_kernel, n_blocks), out_shape=jax.Sh...  11.3 us
    pallas_call x3, Pallas kernels, split(): pl.pallas_call(functools.partial(split_kernel, width), out_shape=(out,) *...  9.68 us
    dynamic_slice x5, local copies, waits for them, and re-layouts, wall_rows(): lax.dynamic_index_in_dim(blocks, index ^ k, 0, False)  8.3 us
  transfers between devices with their start and end apart: 24, of which 11 were waited for; matrix products, arithmetic and copies ran while one was open for 14% of the time, Pallas kernels for 19%

commit v1 on v0

--- a/solution.py
+++ b/solution.py
@@ -35,7 +35,7 @@
 
 
 def params():
-    return pltpu.CompilerParams(vmem_limit_bytes=40 << 20)
+    return pltpu.CompilerParams(vmem_limit_bytes=20 << 20)
 
 
 SMEM = pl.BlockSpec(memory_space=pltpu.SMEM)
@@ -79,7 +79,7 @@
     )(x)
 
 
-def join(width, sol_parts, res_parts, sol_ref, res_ref):
+def join(width, sol_parts, res_parts, sol_ref, res_ref, begin, end):
     chunks = len(sol_parts)
     cw = width // chunks
     half = cw // 2
@@ -103,7 +103,7 @@
         res_ref[LANES:, lanes] = both[HALF:]
         return 0
 
-    lax.fori_loop(0, sol_ref.shape[1] // LANES, step, 0)
+    lax.fori_loop(begin, end, step, 0, unroll=2)
 
 
 UNROLL = 4
@@ -210,7 +210,7 @@
     return top, low.reshape(points, half, LANES)
 
 
-def wall_kernel(n_blocks, f_ref, mh_ref, ml_ref, *rest):
+def wall_kernel(n_blocks, f_ref, s_ref, mh_ref, ml_ref, *rest):
     blocks = rest[:n_blocks]
     out_ref, high_ref, low_ref = rest[n_blocks:]
     points, rows, _ = f_ref.shape
@@ -220,61 +220,71 @@
         stage(high_ref, low_ref, 2 * LANES * k, ref, cw)
     result = product(high_ref[...], low_ref[...], mh_ref[...], ml_ref[...])
     top, low = unstage(result, points, cw)
-    out_ref[:, :half, :] = f_ref[:, :half, :] - top[0]
-    out_ref[:, half:cw, :] = f_ref[:, half:cw, :] - top[1]
-    out_ref[:, cw:, :] = f_ref[:, cw:, :] - low
-
-
-def wall(f, mh, ml, blocks):
+    out_ref[:, :half, :] = f_ref[:, :half, :] - s_ref[:, :half, :] - top[0]
+    out_ref[:, half:cw, :] = f_ref[:, half:cw, :] - s_ref[:, half:cw, :] - top[1]
+    out_ref[:, cw:, :] = f_ref[:, cw:, :] - s_ref[:, cw:, :] - low
+
+
+def wall(f, s, mh, ml, blocks):
     points, rows, _ = f.shape
     n_blocks = len(blocks)
     m_rows = points * rows * 2 // 3
     return pl.pallas_call(
         functools.partial(wall_kernel, n_blocks),
         out_shape=jax.ShapeDtypeStruct(f.shape, f.dtype),
-        in_specs=[VMEM] * (3 + n_blocks),
+        in_specs=[VMEM] * (4 + n_blocks),
         out_specs=VMEM,
         scratch_shapes=[pltpu.VMEM((m_rows, 2 * LANES * n_blocks), jnp.bfloat16)] * 2,
         compiler_params=params(),
         cost_estimate=pl.CostEstimate(flops=3000000000, bytes_accessed=8 * f.size * 4, transcendentals=0),
         name="wall",
-    )(f, mh, ml, *blocks)
-
-
-def last_kernel(bands, width, n_earlier, off_ref, sign_ref, g_ref, s_ref, t_ref, x_ref, far_ref, w_ref, bh_ref, bl_ref, *rest):
+    )(f, s, mh, ml, *blocks)
+
+
+def last_kernel(bands, width, n_earlier, off_ref, sign_ref, g_ref, t_ref, x_ref, far_ref, w_ref, bh_ref, bl_ref, *rest):
     earlier = rest[: 2 * n_earlier]
     rest = rest[2 * n_earlier :]
     if width:
-        sol_ref, res_ref, ext_ref, high_ref, low_ref, x_new_ref, r_ref = rest
+        sol_hbm, res_hbm, high_ref, low_ref, x_new_ref, r_ref, sol_ref, res_ref, sems = rest
     else:
-        x_new_ref, r_ref, ext_ref, high_ref, low_ref = rest
+        x_new_ref, r_ref, high_ref, low_ref = rest
     points, rows, _ = x_ref.shape
     cw = rows * 2 // 3
     half = cw // 2
     sign = sign_ref[0]
-    fill(ext_ref, [(far_ref, 1)], points)
 
     def begin(i, _):
         here = pl.ds(i * UNROLL, UNROLL)
-        r_ref[here] = g_ref[here] - s_ref[here] - t_ref[here]
+        r_ref[here] = g_ref[here] - t_ref[here]
         return 0
 
     lax.fori_loop(0, points // UNROLL, begin, 0)
-    for b in range(bands):
-        start = off_ref[b] + 2 * sign * points
-
-        @pl.when(jnp.logical_and(start > -points, start < points))
-        def _():
-            def step(i, _):
-                for u in range(UNROLL):
-                    p = i * UNROLL + u
-                    top, low = scaled(w_ref, b * points + p, ext_ref[points + start + p], cw)
-                    r_ref[p, :cw, :] = r_ref[p, :cw, :] - top
-                    r_ref[p, cw:, :] = r_ref[p, cw:, :] - low
-                return 0
-
-            lax.fori_loop(0, points // UNROLL, step, 0)
-
+
+    def band(b, _):
+        shift = off_ref[b] + 2 * sign * points
+        first = jnp.maximum(0, -shift)
+        count = points - jnp.abs(shift)
+
+        def point(p):
+            top, low = scaled(w_ref, b * points + p, far_ref[p + shift], cw)
+            r_ref[p, :cw, :] = r_ref[p, :cw, :] - top
+            r_ref[p, cw:, :] = r_ref[p, cw:, :] - low
+
+        def several(i, _):
+            for u in range(UNROLL):
+                point(first + i * UNROLL + u)
+            return 0
+
+        def one(i, _):
+            point(first + i)
+            return 0
+
+        groups = jnp.maximum(count, 0) // UNROLL
+        lax.fori_loop(0, groups, several, 0)
+        lax.fori_loop(groups * UNROLL, count, one, 0)
+        return 0
+
+    lax.fori_loop(0, bands, band, 0)
     stage(high_ref, low_ref, 0, r_ref, cw)
     result = product(high_ref[...], low_ref[...], bh_ref[...], bl_ref[...])
     top, low = unstage(result, points, cw)
@@ -282,59 +292,109 @@
     x_new_ref[:, half:cw, :] = x_ref[:, half:cw, :] + top[1]
     x_new_ref[:, cw:, :] = x_ref[:, cw:, :] + low
     if width:
-        join(width, [*earlier[::2], x_new_ref], [*earlier[1::2], r_ref], sol_ref, res_ref)
-
-
-def last(offsets, sign, g, s, t, x, second, w, bh, bl, earlier, width):
+        slabs = sems.shape[1]
+        wide = sol_ref.shape[1] // slabs
+
+        def copies(n):
+            at = pl.ds(pl.multiple_of(n * wide, LANES), wide)
+            return [
+                pltpu.make_async_copy(ref.at[:, at], hbm.at[:, at], sems.at[which, n])
+                for which, (ref, hbm) in enumerate(((sol_ref, sol_hbm), (res_ref, res_hbm)))
+            ]
+
+        for n in range(slabs):
+            join(width, [*earlier[::2], x_new_ref], [*earlier[1::2], r_ref], sol_ref, res_ref, n * wide // LANES, (n + 1) * wide // LANES)
+            for copy in copies(n):
+                copy.start()
+        for n in range(slabs):
+            for copy in copies(n):
+                copy.wait()
+
+
+SLABS = 4
+
+
+def last(offsets, sign, g, t, x, second, w, bh, bl, earlier, width):
     bands = offsets.shape[0]
     points, rows, _ = x.shape
     chunk = pltpu.VMEM(x.shape, jnp.float32)
-    if width:
-        out = jax.ShapeDtypeStruct((LANES + HALF, points * width), x.dtype)
-    else:
-        out = jax.ShapeDtypeStruct(x.shape, x.dtype)
+    shape = (LANES + HALF, points * width) if width else x.shape
+    out = jax.ShapeDtypeStruct(shape, x.dtype)
     m_rows = points * rows * 2 // 3
+    whole = pltpu.VMEM(shape, jnp.float32)
     return pl.pallas_call(
         functools.partial(last_kernel, bands, width, len(earlier) // 2),
         out_shape=(out, out),
-        in_specs=[SMEM, SMEM] + [VMEM] * (8 + len(earlier)),
-        out_specs=(VMEM, VMEM),
+        in_specs=[SMEM, SMEM] + [VMEM] * (7 + len(earlier)),
+        out_specs=(pl.BlockSpec(memory_space=pltpu.HBM) if width else VMEM,) * 2,
         scratch_shapes=[
-            pltpu.VMEM((3 * points, rows, LANES), jnp.float32),
             pltpu.VMEM((m_rows, 2 * LANES), jnp.bfloat16),
             pltpu.VMEM((m_rows, 2 * LANES), jnp.bfloat16),
         ]
-        + ([chunk, chunk] if width else []),
+        + ([chunk, chunk, whole, whole, pltpu.SemaphoreType.DMA((2, SLABS))] if width else []),
         compiler_params=params(),
         cost_estimate=pl.CostEstimate(flops=1000000000, bytes_accessed=8 * x.size * 4, transcendentals=0),
         name="last",
-    )(offsets, sign, g, s, t, x, second, w, bh, bl, *earlier)
-
-
-def two_parts(value):
-    high = lax.reduce_precision(value, 8, 7)
-    return high.astype(jnp.bfloat16), (value - high).astype(jnp.bfloat16)
-
-
-def right_side(matrix):
-    rows = matrix.shape[0]
-    return jnp.pad(matrix.T, ((0, 2 * LANES - rows), (0, 2 * LANES - rows)))
-
-
-def wall_rows(wall_even, wall_odd, rows):
+    )(offsets, sign, g, t, x, second, w, bh, bl, *earlier)
+
+
+def flip_matrix(rows, turned):
+    size = 2 * LANES
+    i = lax.broadcasted_iota(jnp.int32, (size, size), 0)
+    j = lax.broadcasted_iota(jnp.int32, (size, size), 1)
+    target = jnp.where(turned, rows - 1 - i, i)
+    return jnp.where(jnp.logical_and(j == target, i < rows), 1.0, 0.0).astype(jnp.bfloat16)
+
+
+def prep_kernel(count, index_ref, even_ref, odd_ref, inv_ref, mh_ref, ml_ref, bh_ref, bl_ref, pad_ref):
+    rows = inv_ref.shape[0]
+    size = 2 * LANES
+    index = index_ref[0]
+    half = count // 2
+    lower = index >= half
+    at = pl.ds(pl.multiple_of(jnp.where(lower, count - 1 - index, index) * rows, 8), rows)
+    pad_ref[...] = jnp.zeros_like(pad_ref)
+
+    def transposed(value):
+        pad_ref[:rows, :rows] = value
+        return pad_ref[...].T
+
+    high, low = halves(transposed(inv_ref[...]))
+    bh_ref[...] = high
+    bl_ref[...] = low
+    keep_or_turn = flip_matrix(rows, lower)
+    turn = flip_matrix(rows, True)
+    dot = functools.partial(jnp.dot, preferred_element_type=jnp.float32)
+    even = even_ref[at, :]
+    odd = odd_ref[at, :]
+    for j in range(count):
+        block = j if j < half else count - 1 - j
+        columns = slice(block * rows, (block + 1) * rows)
+        weight = jnp.where(lower == (j >= half), 0.5, -0.5)
+        parts = halves(transposed(0.5 * even[:, columns] + weight * odd[:, columns]))
+        place = pl.ds(pl.multiple_of(jnp.bitwise_xor(index, j) * size, size), size)
+        for out_ref, part in zip((mh_ref, ml_ref), parts):
+            if j >= half:
+                part = dot(turn, part).astype(jnp.bfloat16)
+            out_ref[place, :] = dot(part, keep_or_turn).astype(jnp.bfloat16)
+
+
+def prep(wall_even, wall_odd, block_inv):
     count = lax.axis_size("wall")
-    index = lax.axis_index("wall")
-    upper = index < count // 2
-    at = jnp.where(upper, index, count - 1 - index) * rows
-    even = lax.dynamic_slice_in_dim(wall_even, at, rows, 0)
-    odd = lax.dynamic_slice_in_dim(wall_odd, at, rows, 0)
-    same = 0.5 * (even + odd)
-    cross = 0.5 * (even - odd)
-    full = jnp.concatenate([same, jnp.flip(cross, 1)], 1)
-    full = jnp.where(upper, full, jnp.flip(full, (0, 1)))
-    blocks = jnp.stack([right_side(full[:, k * rows : (k + 1) * rows]) for k in range(count)])
-    ordered = jnp.concatenate([lax.dynamic_index_in_dim(blocks, index ^ k, 0, False) for k in range(count)], 0)
-    return two_parts(ordered)
+    index = lax.axis_index("wall").astype(jnp.int32)[None]
+    size = 2 * LANES
+    m = jax.ShapeDtypeStruct((count * size, size), jnp.bfloat16)
+    b = jax.ShapeDtypeStruct((size, size), jnp.bfloat16)
+    return pl.pallas_call(
+        functools.partial(prep_kernel, count),
+        out_shape=(m, m, b, b),
+        in_specs=[SMEM, VMEM, VMEM, VMEM],
+        out_specs=(VMEM,) * 4,
+        scratch_shapes=[pltpu.VMEM((size, size), jnp.float32)],
+        compiler_params=params(),
+        cost_estimate=pl.CostEstimate(flops=600000000, bytes_accessed=3000000, transcendentals=0),
+        name="prep",
+    )(index, wall_even, wall_odd, block_inv)
 
 
 def after(value, *others):
@@ -357,8 +417,7 @@
     low = weights[:, LANES:]
     own_w = jnp.stack([weights[:, :LANES], jnp.concatenate([low, low], 1)])
     their_w = partner(own_w[:, : bands * points])
-    mh, ml = wall_rows(wall_even, wall_odd, rows)
-    bh, bl = two_parts(right_side(block_inv))
+    mh, ml, bh, bl = prep(wall_even, wall_odd, block_inv)
     f = split(forcing, chunks, points)
     residual = [None] * chunks
     arrived = raw_first
@@ -392,24 +451,11 @@
             theirs.append(partner(partial))
         new = []
         for k in range(chunks):
-            g = wall(f[k], mh, ml, walls[k])
+            g = wall(f[k], sums[k], mh, ml, walls[k])
             final = final_sweep and k == chunks - 1
             earlier = [a for pair in new for a in pair] if final else []
             new.append(
-                last(
-                    offsets,
-                    sign,
-                    g,
-                    sums[k],
-                    theirs[k],
-                    state[k],
-                    seconds[k],
-                    own_w,
-                    bh,
-                    bl,
-                    earlier,
-                    width if final else 0,
-                )
+                last(offsets, sign, g, theirs[k], state[k], seconds[k], own_w, bh, bl, earlier, width if final else 0)
             )
         state = [pair[0] for pair in new]
         residual = [pair[1] for pair in new]

time: 197 us -> 194 us (0.985)
  waiting for transfers between devices: 102 us -> 127 us
  local copies, waits for them, and re-layouts: 21.1 us -> 3.28 us
  other arithmetic: 8.57 us -> 2.24 us
  Pallas kernels: 48.3 us -> 45.3 us
    ppermute x12, waiting for transfers between devices: 37.5 us -> 53.7 us  [exchange(): return lax.ppermute(value, 'wall', [(i, i ^ bit) for i in range(count)])]
    dynamic_slice x5 -> x0, local copies, waits for them, and re-layouts: 8.3 us -> none  [wall_rows(): lax.dynamic_index_in_dim(blocks, index ^ k, 0, False)]
    ppermute x7, waiting for transfers between devices: 30.3 us -> 37.8 us  [far(): return lax.ppermute(value, 'span', pairs)]
    rev x1 -> x0, local copies, waits for them, and re-layouts: 7.07 us -> none  [wall_rows(): full = jnp.where(upper, full, jnp.flip(full, (0, 1)))]
    ppermute x7, starting transfers between devices: 7.88 us -> 5.51 us  [far(): return lax.ppermute(value, 'span', pairs)]
    ppermute x5, starting transfers between devices: 2.59 us -> 4.89 us  [partner(): return lax.ppermute(value, 'span', [(i, i ^ 1) for i in range(count)])]
    pallas_call x4, Pallas kernels: 14.4 us -> 12.1 us  [last(): pl.pallas_call(functools.partial(last_kernel, bands, width, len(earlier)...]
  transfers between devices with their start and end apart: 24 -> 24, of which waited for: 11 -> 12; matrix products, arithmetic and copies ran while one was open for 14% -> 1% of each run, Pallas kernels for 19% -> 21%
where the time goes in v1:
time: 194 us
  waiting for transfers between devices  127 us (65%)
  Pallas kernels  45.3 us (23%)
  starting transfers between devices  15.5 us (8%)
  local copies, waits for them, and re-layouts  3.28 us (2%)
  other arithmetic  2.24 us (1%)
    ppermute x12, waiting for transfers between devices, exchange(): return lax.ppermute(value, 'wall', [(i, i ^ bit) for i in range(count)])  53.7 us
    ppermute x7, waiting for transfers between devices, far(): return lax.ppermute(value, 'span', pairs)  37.8 us
    ppermute x5, waiting for transfers between devices, partner(): return lax.ppermute(value, 'span', [(i, i ^ 1) for i in range(count)])  35.2 us
    pallas_call x4, Pallas kernels, near(): pl.pallas_call(functools.partial(near_kernel, bands), out_shape=(out, out...  13 us
    pallas_call x4, Pallas kernels, last(): pl.pallas_call(functools.partial(last_kernel, bands, width, len(earlier)...  12.1 us
    pallas_call x4, Pallas kernels, wall(): pl.pallas_call(functools.partial(wall_kernel, n_blocks), out_shape=jax.Sh...  11.2 us
    pallas_call x3, Pallas kernels, split(): pl.pallas_call(functools.partial(split_kernel, width), out_shape=(out,) *...  7.98 us
    ppermute x7, starting transfers between devices, far(): return lax.ppermute(value, 'span', pairs)  5.51 us
  transfers between devices with their start and end apart: 24, of which 12 were waited for; matrix products, arithmetic and copies ran while one was open for 1% of the time, Pallas kernels for 21%

profile of v1, /device:TPU:20, one launch (start us, length us, event | category | flops | bytes accessed | tf_op | source)
XLA Modules:
  0.0 194.2 jit_solution(17613141028345339319)
XLA Ops:
  0.6 0.5 collective-permute-start
  1.1 1.4 copy-done
  2.6 3.3 %split.4 = (f32[64,24,128]{2,1,0:T(8,128)S(1)}, f32[64,24,128]{2,1,0:T(8,128)}) custom-call(f32[192,2048]{1,0:T(8,128)S(1)} %copy-done), custom_call_target="tpu_custom_call" | custom-call | bytes 3145728 | tf_op jit(solution)/shard_map/split/pallas_call | solution.py:71
  5.8 0.5 collective-permute-start.14
  6.3 1.5 collective-permute-start.3
  7.9 0.5 collective-permute-start.2
  8.8 17.6 %collective-permute-done.14.rest_2_ = f32[64,24,128]{2,1,0:T(8,128)} collective-permute-done((f32[64,24,128]{2,1,0:T(8,128)S(1)}, f32[64,24,128]{2,1,0:T(8,128)}, u32[]{:S(2)}, u32[]{:S(2)}) %collective-permute-start.14) | collective-permute-done | bytes 786464 | tf_op jit(solution)/shard_map/ppermute | solution.py:20
  26.4 0.8 fusion
  27.2 14.6 %collective-permute-done.3.rest_2_ = f32[64,24,128]{2,1,0:T(8,128)} collective-permute-done((f32[64,24,128]{2,1,0:T(8,128)}, f32[64,24,128]{2,1,0:T(8,128)}, u32[]{:S(2)}, u32[]{:S(2)}) %collective-permute-start.3) | collective-permute-done | bytes 786464 | tf_op jit(solution)/shard_map/ppermute | solution.py:20
  41.8 2.6 %collective-permute-start.1 = (f32[2,512,128]{2,1,0:T(8,128)}, f32[2,512,128]{2,1,0:T(8,128)S(1)}, u32[]{:S(2)}, u32[]{:S(2)}) collective-permute-start(f32[2,512,128]{2,1,0:T(8,128)} %fusion), channel_id=1, source_target_pairs={{0,4},{4,0},{8,12},{12,8},{16,20},{20,16},{24,28},{28,24},{1,5},{5... | collective-permute-start | bytes 1572872 | tf_op jit(solution)/shard_map/ppermute | solution.py:25
  44.5 1.1 pad_maximum_fusion.w_ref
  45.5 2.4 %split.5 = (f32[64,24,128]{2,1,0:T(8,128)S(1)}, f32[64,24,128]{2,1,0:T(8,128)S(1)}) custom-call(f32[192,2048]{1,0:T(8,128)S(1)} %collective-permute-done.x_ref), custom_call_target="tpu_custom_call" | custom-call | bytes 3145728 | tf_op jit(solution)/shard_map/split/pallas_call | solution.py:71
  47.9 7.5 %collective-permute-done.1.theirs_ref = f32[2,512,128]{2,1,0:T(8,128)S(1)} collective-permute-done((f32[2,512,128]{2,1,0:T(8,128)}, f32[2,512,128]{2,1,0:T(8,128)S(1)}, u32[]{:S(2)}, u32[]{:S(2)}) %collective-permute-start.1) | collective-permute-done | bytes 524320 | tf_op jit(solution)/shard_map/ppermute | solution.py:25
  55.4 4.3 %near.4 = (f32[64,24,128]{2,1,0:T(8,128)}, f32[64,24,128]{2,1,0:T(8,128)S(1)}) custom-call(s32[8]{0:T(128)S(1)} %copy-done.2, s32[1]{0:T(128)} %bitcast.sign_ref, f32[64,24,128]{2,1,0:T(8,128)} %get-tuple-element.37.x_ref.rest_0_, f32[64,24,128]{2,1,0:T(8,128)S(1)} %get-tuple-element.32.far_ref, f32[2,576,128]{2,1,0:T(8,128)S(1)} %pad_maximum_fusion.w_ref, ...), custom_call_target="tpu_custom_call" | custom-call | flops 1000000000 | bytes 4718592 | tf_op jit(solution)/shard_map/near/pallas_call | solution.py:166
  59.7 0.9 copy-done.8
  60.6 1.7 collective-permute-start.5
  62.3 0.3 collective-permute-start.6
  62.7 3.5 %near.6 = (f32[64,24,128]{2,1,0:T(8,128)}, f32[64,24,128]{2,1,0:T(8,128)S(1)}) custom-call(s32[8]{0:T(128)S(1)} %copy-done.2, s32[1]{0:T(128)} %bitcast.sign_ref, f32[64,24,128]{2,1,0:T(8,128)S(1)} %get-tuple-element.50.x_ref.rest_0_, f32[64,24,128]{2,1,0:T(8,128)S(1)} %get-tuple-element.47.far_ref, f32[2,576,128]{2,1,0:T(8,128)S(1)} %pad_maximum_fusion.w_ref, ...), custom_call_target="tpu_custom_call" | custom-call | flops 1000000000 | bytes 4718592 | tf_op jit(solution)/shard_map/near/pallas_call | solution.py:166
  66.1 0.9 copy-done.10
  67.0 0.4 collective-permute-start.16
  67.4 1.9 %collective-permute-start.17 = (f32[64,24,128]{2,1,0:T(8,128)S(1)}, f32[64,24,128]{2,1,0:T(8,128)}, u32[]{:S(2)}, u32[]{:S(2)}) collective-permute-start(f32[64,24,128]{2,1,0:T(8,128)S(1)} %get-tuple-element.50.x_ref.rest_0_), channel_id=1, source_target_pairs={{0,8},{4,28},{8,16},{12,4},{16,24},{20,12},{24,0},{28,20},{1,9},{5... | collective-permute-start | bytes 2359304 | tf_op jit(solution)/shard_map/ppermute | solution.py:34
  69.4 2.4 %split.3 = (f32[64,24,128]{2,1,0:T(8,128)S(1)}, f32[64,24,128]{2,1,0:T(8,128)S(1)}) custom-call(f32[192,2048]{1,0:T(8,128)S(1)} %copy-done.1), custom_call_target="tpu_custom_call" | custom-call | bytes 3145728 | tf_op jit(solution)/shard_map/split/pallas_call | solution.py:71
  71.8 1.0 prep.1
  72.8 3.6 %wall.6.g_ref = f32[64,24,128]{2,1,0:T(8,128)S(1)} custom-call(f32[64,24,128]{2,1,0:T(8,128)S(1)} %get-tuple-element.45.f_ref, f32[64,24,128]{2,1,0:T(8,128)S(1)} %copy-done.11, bf16[1024,256]{1,0:T(8,128)(2,1)S(1)} %get-tuple-element.34.mh_ref, bf16[1024,256]{1,0:T(8,128)(2,1)S(1)} %get-tuple-element.35.ml_ref, ...), custom_call_target="tpu_custom_call" | custom-call | flops 3000000000 | bytes 6291456 | tf_op jit(solution)/shard_map/wall/pallas_call | solution.py:232
  76.5 3.8 %wall.4.g_ref = f32[64,24,128]{2,1,0:T(8,128)S(1)} custom-call(f32[64,24,128]{2,1,0:T(8,128)S(1)} %get-tuple-element.30.f_ref, f32[64,24,128]{2,1,0:T(8,128)S(1)} %copy-done.9, bf16[1024,256]{1,0:T(8,128)(2,1)S(1)} %get-tuple-element.34.mh_ref, bf16[1024,256]{1,0:T(8,128)(2,1)S(1)} %get-tuple-element.35.ml_ref, ...), custom_call_target="tpu_custom_call" | custom-call | flops 3000000000 | bytes 6291456 | tf_op jit(solution)/shard_map/wall/pallas_call | solution.py:232
  80.2 1.0 collective-permute-done.5.t_ref
  81.3 1.7 collective-permute-done.6.far_ref
  83.0 3.0 %last.4 = (f32[64,24,128]{2,1,0:T(8,128)S(1)}, f32[64,24,128]{2,1,0:T(8,128)}) custom-call(s32[8]{0:T(128)S(1)} %copy-done.2, s32[1]{0:T(128)} %bitcast.sign_ref, f32[64,24,128]{2,1,0:T(8,128)S(1)} %wall.4.g_ref, f32[64,24,128]{2,1,0:T(8,128)} %collective-permute-done.5.t_ref, f32[64,24,128]{2,1,0:T(8,128)} %get-tuple-element.37.x_ref.rest_0_, ...), custom_call_target="tpu_custom_call" | custom-call | flops 1000000000 | bytes 6291456 | tf_op jit(solution)/shard_map/last/pallas_call | solution.py:325
  86.1 0.4 collective-permute-start.7
  86.5 8.8 %collective-permute-done.16.t_ref = f32[64,24,128]{2,1,0:T(8,128)} collective-permute-done((f32[64,24,128]{2,1,0:T(8,128)}, f32[64,24,128]{2,1,0:T(8,128)}, u32[]{:S(2)}, u32[]{:S(2)}) %collective-permute-start.16) | collective-permute-done | bytes 786464 | tf_op jit(solution)/shard_map/ppermute | solution.py:25
  95.3 31.6 %collective-permute-done.17.far_ref = f32[64,24,128]{2,1,0:T(8,128)} collective-permute-done((f32[64,24,128]{2,1,0:T(8,128)S(1)}, f32[64,24,128]{2,1,0:T(8,128)}, u32[]{:S(2)}, u32[]{:S(2)}) %collective-permute-start.17) | collective-permute-done | bytes 786464 | tf_op jit(solution)/shard_map/ppermute | solution.py:34
  126.8 2.8 %last.5 = (f32[64,24,128]{2,1,0:T(8,128)S(1)}, f32[64,24,128]{2,1,0:T(8,128)}) custom-call(s32[8]{0:T(128)S(1)} %copy-done.2, s32[1]{0:T(128)} %bitcast.sign_ref, f32[64,24,128]{2,1,0:T(8,128)S(1)} %wall.6.g_ref, f32[64,24,128]{2,1,0:T(8,128)} %collective-permute-done.16.t_ref, f32[64,24,128]{2,1,0:T(8,128)S(1)} %get-tuple-element.50.x_ref.rest_0_, ...), custom_call_target="tpu_custom_call" | custom-call | flops 1000000000 | bytes 6291456 | tf_op jit(solution)/shard_map/last/pallas_call | solution.py:325
  129.7 0.5 collective-permute-start.20
  130.2 1.5 collective-permute-start.9
  131.7 2.0 %collective-permute-start.23 = (f32[64,24,128]{2,1,0:T(8,128)S(1)}, f32[64,24,128]{2,1,0:T(8,128)S(1)}, u32[]{:S(2)}, u32[]{:S(2)}) collective-permute-start(f32[64,24,128]{2,1,0:T(8,128)S(1)} %get-tuple-element.55.x_ref.rest_0_), channel_id=1, source_target_pairs={{0,8},{4,28},{8,16},{12,4},{16,24},{20,12},{24,0},{28,20},{1,9},{5... | collective-permute-start | bytes 2359304 | tf_op jit(solution)/shard_map/ppermute | solution.py:34
  133.7 16.3 %collective-permute-done.20.rest_2_ = f32[64,24,128]{2,1,0:T(8,128)S(1)} collective-permute-done((f32[64,24,128]{2,1,0:T(8,128)S(1)}, f32[64,24,128]{2,1,0:T(8,128)S(1)}, u32[]{:S(2)}, u32[]{:S(2)}) %collective-permute-start.20) | collective-permute-done | bytes 786464 | tf_op jit(solution)/shard_map/ppermute | solution.py:20
  150.0 2.6 %near.7 = (f32[64,24,128]{2,1,0:T(8,128)S(1)}, f32[64,24,128]{2,1,0:T(8,128)S(1)}) custom-call(s32[8]{0:T(128)S(1)} %copy-done.2, s32[1]{0:T(128)} %bitcast.sign_ref, f32[64,24,128]{2,1,0:T(8,128)S(1)} %get-tuple-element.55.x_ref.rest_0_, f32[64,24,128]{2,1,0:T(8,128)S(1)} %collective-permute-done.18.far_ref, f32[2,576,128]{2,1,0:T(8,128)S(1)} %pad_maximum_fusion.w_ref, ...), custom_call_target="tpu_custom_call" | custom-call | flops 1000000000 | bytes 4718592 | tf_op jit(solution)/shard_map/near/pallas_call | solution.py:166
  152.7 0.6 collective-permute-start.8
  153.3 5.2 %collective-permute-done.9.rest_2_ = f32[64,24,128]{2,1,0:T(8,128)S(1)} collective-permute-done((f32[64,24,128]{2,1,0:T(8,128)S(1)}, f32[64,24,128]{2,1,0:T(8,128)S(1)}, u32[]{:S(2)}, u32[]{:S(2)}) %collective-permute-start.9) | collective-permute-done | bytes 786464 | tf_op jit(solution)/shard_map/ppermute | solution.py:20
  158.5 2.6 %near.5 = (f32[64,24,128]{2,1,0:T(8,128)S(1)}, f32[64,24,128]{2,1,0:T(8,128)S(1)}) custom-call(s32[8]{0:T(128)S(1)} %copy-done.2, s32[1]{0:T(128)} %bitcast.sign_ref, f32[64,24,128]{2,1,0:T(8,128)S(1)} %get-tuple-element.44.x_ref.rest_0_, f32[64,24,128]{2,1,0:T(8,128)S(1)} %collective-permute-done.7.far_ref, f32[2,576,128]{2,1,0:T(8,128)S(1)} %pad_maximum_fusion.w_ref, ...), custom_call_target="tpu_custom_call" | custom-call | flops 1000000000 | bytes 4718592 | tf_op jit(solution)/shard_map/near/pallas_call | solution.py:166
  161.1 0.2 collective-permute-start.12
  161.5 1.9 wall.7.g_ref
  163.4 9.7 %collective-permute-done.22.t_ref = f32[64,24,128]{2,1,0:T(8,128)S(1)} collective-permute-done((f32[64,24,128]{2,1,0:T(8,128)S(1)}, f32[64,24,128]{2,1,0:T(8,128)S(1)}, u32[]{:S(2)}, u32[]{:S(2)}) %collective-permute-start.22) | collective-permute-done | bytes 786464 | tf_op jit(solution)/shard_map/ppermute | solution.py:25
  173.1 1.7 last.6
  174.9 1.9 wall.5.g_ref
  176.8 4.5 %collective-permute-done.12.far_ref = f32[64,24,128]{2,1,0:T(8,128)S(1)} collective-permute-done((f32[64,24,128]{2,1,0:T(8,128)S(1)}, f32[64,24,128]{2,1,0:T(8,128)S(1)}, u32[]{:S(2)}, u32[]{:S(2)}) %collective-permute-start.12) | collective-permute-done | bytes 786464 | tf_op jit(solution)/shard_map/ppermute | solution.py:34
  181.3 8.2 %collective-permute-done.11.t_ref = f32[64,24,128]{2,1,0:T(8,128)S(1)} collective-permute-done((f32[64,24,128]{2,1,0:T(8,128)S(1)}, f32[64,24,128]{2,1,0:T(8,128)S(1)}, u32[]{:S(2)}, u32[]{:S(2)}) %collective-permute-start.11) | collective-permute-done | bytes 786464 | tf_op jit(solution)/shard_map/ppermute | solution.py:25
  189.5 4.5 %last.7 = (f32[192,2048]{1,0:T(8,128)}, f32[192,2048]{1,0:T(8,128)}) custom-call(s32[8]{0:T(128)S(1)} %copy-done.2, s32[1]{0:T(128)} %bitcast.sign_ref, f32[64,24,128]{2,1,0:T(8,128)S(1)} %wall.5.g_ref, f32[64,24,128]{2,1,0:T(8,128)S(1)} %collective-permute-done.11.t_ref, f32[64,24,128]{2,1,0:T(8,128)S(1)} %get-tuple-element.44.x_ref.rest_0_, ...), custom_call_target="tpu_custom_call" | custom-call | flops 1000000000 | bytes 6291456 | tf_op jit(solution)/shard_map/last/pallas_call | solution.py:325
  (57 shorter events, 0.6 us)
Async XLA Ops:
  0.6 43.8 %collective-permute-start = (f32[192,2048]{1,0:T(8,128)}, f32[192,2048]{1,0:T(8,128)S(1)}, u32[]{:S(2)}, u32[]{:S(2)}) collective-permute-start(f32[192,2048]{1,0:T(8,128)} %x_ref.3), channel_id=1, source_target_pairs={{0,24},{4,12},{8,0},{12,20},{16,8},{20,28},{24,16},{28,4},{1,25},{... | collective-permute-start | bytes 4718600 | tf_op jit(solution)/shard_map/ppermute | solution.py:34
  1.1 1.4 copy-start
  2.6 5.8 %copy-start.16 = (s32[8,64]{1,0:T(8,128)S(1)}, s32[8,64]{1,0:T(8,128)}, u32[]{:S(2)}) copy-start(s32[8,64]{1,0:T(8,128)} %param.16) | copy-start | bytes 6148
  2.6 5.8 %copy-start.14 = (f32[8,192,64]{1,2,0:T(8,128)S(1)}, f32[8,192,64]{1,2,0:T(8,128)}, u32[]{:S(2)}) copy-start(f32[8,192,64]{1,2,0:T(8,128)} %param.14) | copy-start | bytes 1179652
  2.6 5.9 %copy-start.15 = (f32[192,64]{0,1:T(8,128)S(1)}, f32[192,64]{0,1:T(8,128)}, u32[]{:S(2)}) copy-start(f32[192,64]{0,1:T(8,128)} %param.13) | copy-start | bytes 147460
  5.8 20.5 %collective-permute-start.14 = (f32[64,24,128]{2,1,0:T(8,128)S(1)}, f32[64,24,128]{2,1,0:T(8,128)}, u32[]{:S(2)}, u32[]{:S(2)}) collective-permute-start(f32[64,24,128]{2,1,0:T(8,128)S(1)} %get-tuple-element.50.x_ref.rest_0_), channel_id=1, source_target_pairs={{0,2},{1,3},{2,0},{3,1},{4,6},{5,7},{6,4},{7,5},{8,10},{9,11},{10,... | collective-permute-start | bytes 2359304 | tf_op jit(solution)/shard_map/ppermute | solution.py:20
  6.3 35.5 %collective-permute-start.3 = (f32[64,24,128]{2,1,0:T(8,128)}, f32[64,24,128]{2,1,0:T(8,128)}, u32[]{:S(2)}, u32[]{:S(2)}) collective-permute-start(f32[64,24,128]{2,1,0:T(8,128)} %get-tuple-element.37.x_ref.rest_0_), channel_id=1, source_target_pairs={{0,2},{1,3},{2,0},{3,1},{4,6},{5,7},{6,4},{7,5},{8,10},{9,11},{10,... | collective-permute-start | bytes 2359304 | tf_op jit(solution)/shard_map/ppermute | solution.py:20
  7.9 54.4 %collective-permute-start.13 = (f32[64,24,128]{2,1,0:T(8,128)S(1)}, f32[64,24,128]{2,1,0:T(8,128)}, u32[]{:S(2)}, u32[]{:S(2)}) collective-permute-start(f32[64,24,128]{2,1,0:T(8,128)S(1)} %get-tuple-element.50.x_ref.rest_0_), channel_id=1, source_target_pairs={{0,1},{1,0},{2,3},{3,2},{4,5},{5,4},{6,7},{7,6},{8,9},{9,8},{10,11... | collective-permute-start | bytes 2359304 | tf_op jit(solution)/shard_map/ppermute | solution.py:20
  7.9 59.2 %collective-permute-start.2 = (f32[64,24,128]{2,1,0:T(8,128)}, f32[64,24,128]{2,1,0:T(8,128)}, u32[]{:S(2)}, u32[]{:S(2)}) collective-permute-start(f32[64,24,128]{2,1,0:T(8,128)} %get-tuple-element.37.x_ref.rest_0_), channel_id=1, source_target_pairs={{0,1},{1,0},{2,3},{3,2},{4,5},{5,4},{6,7},{7,6},{8,9},{9,8},{10,11... | collective-permute-start | bytes 2359304 | tf_op jit(solution)/shard_map/ppermute | solution.py:20
  8.8 35.7 %copy-start.12 = (f32[1,576,128]{2,1,0:T(8,128)}, f32[1,576,128]{2,1,0:T(8,128)S(1)}, u32[]{:S(2)}) copy-start(f32[1,576,128]{2,1,0:T(8,128)S(1)} %get-tuple-element.58) | copy-start | bytes 884740
  8.8 35.7 %copy-start.13 = (f32[1,576,128]{2,1,0:T(8,128)}, f32[1,576,128]{2,1,0:T(8,128)S(1)}, u32[]{:S(2)}) copy-start(f32[1,576,128]{2,1,0:T(8,128)S(1)} %get-tuple-element.59) | copy-start | bytes 884740
  26.4 41.1 %collective-permute-start.15 = (f32[64,24,128]{2,1,0:T(8,128)}, f32[64,24,128]{2,1,0:T(8,128)}, u32[]{:S(2)}, u32[]{:S(2)}) collective-permute-start(f32[64,24,128]{2,1,0:T(8,128)} %collective-permute-done.14.rest_2_), channel_id=1, source_target_pairs={{0,1},{1,0},{2,3},{3,2},{4,5},{5,4},{6,7},{7,6},{8,9},{9,8},{10,11... | collective-permute-start | bytes 2359304 | tf_op jit(solution)/shard_map/ppermute | solution.py:20
  27.2 28.2 %copy-start.2 = (s32[8]{0:T(128)S(1)}, s32[8]{0:T(128)}, u32[]{:S(2)}) copy-start(s32[8]{0:T(128)} %off_ref.15) | copy-start | bytes 100
  41.8 13.6 %collective-permute-start.1 = (f32[2,512,128]{2,1,0:T(8,128)}, f32[2,512,128]{2,1,0:T(8,128)S(1)}, u32[]{:S(2)}, u32[]{:S(2)}) collective-permute-start(f32[2,512,128]{2,1,0:T(8,128)} %fusion), channel_id=1, source_target_pairs={{0,4},{4,0},{8,12},{12,8},{16,20},{20,16},{24,28},{28,24},{1,5},{5... | collective-permute-start | bytes 1572872 | tf_op jit(solution)/shard_map/ppermute | solution.py:25
  44.4 32.0 %collective-permute-start.4 = (f32[64,24,128]{2,1,0:T(8,128)}, f32[64,24,128]{2,1,0:T(8,128)}, u32[]{:S(2)}, u32[]{:S(2)}) collective-permute-start(f32[64,24,128]{2,1,0:T(8,128)} %collective-permute-done.3.rest_2_), channel_id=1, source_target_pairs={{0,1},{1,0},{2,3},{3,2},{4,5},{5,4},{6,7},{7,6},{8,9},{9,8},{10,11... | collective-permute-start | bytes 2359304 | tf_op jit(solution)/shard_map/ppermute | solution.py:20
  55.4 7.2 %copy-start.5 = (f32[2,512,128]{2,1,0:T(8,128)}, f32[2,512,128]{2,1,0:T(8,128)S(1)}, u32[]{:S(2)}) copy-start(f32[2,512,128]{2,1,0:T(8,128)S(1)} %collective-permute-done.1.theirs_ref) | copy-start | bytes 1572868
  59.7 0.9 copy-start.8
  60.6 20.7 %collective-permute-start.5 = (f32[64,24,128]{2,1,0:T(8,128)}, f32[64,24,128]{2,1,0:T(8,128)}, u32[]{:S(2)}, u32[]{:S(2)}) collective-permute-start(f32[64,24,128]{2,1,0:T(8,128)} %get-tuple-element.36), channel_id=1, source_target_pairs={{0,4},{4,0},{8,12},{12,8},{16,20},{20,16},{24,28},{28,24},{1,5},{5... | collective-permute-start | bytes 2359304 | tf_op jit(solution)/shard_map/ppermute | solution.py:25
  62.3 20.7 %collective-permute-start.6 = (f32[64,24,128]{2,1,0:T(8,128)}, f32[64,24,128]{2,1,0:T(8,128)}, u32[]{:S(2)}, u32[]{:S(2)}) collective-permute-start(f32[64,24,128]{2,1,0:T(8,128)} %get-tuple-element.37.x_ref.rest_0_), channel_id=1, source_target_pairs={{0,8},{4,28},{8,16},{12,4},{16,24},{20,12},{24,0},{28,20},{1,9},{5... | collective-permute-start | bytes 2359304 | tf_op jit(solution)/shard_map/ppermute | solution.py:34
  62.7 6.7 %copy-start.1 = (f32[192,2048]{1,0:T(8,128)S(1)}, f32[192,2048]{1,0:T(8,128)}, u32[]{:S(2)}) copy-start(f32[192,2048]{1,0:T(8,128)} %x_ref.2) | copy-start | bytes 4718596
  66.1 0.9 copy-start.10
  67.0 4.7 %copy-start.3 = (f32[384,384]{1,0:T(8,128)S(1)}, f32[384,384]{1,0:T(8,128)}, u32[]{:S(2)}) copy-start(f32[384,384]{1,0:T(8,128)} %even_ref.1) | copy-start | bytes 1769476
  67.0 28.3 %collective-permute-start.16 = (f32[64,24,128]{2,1,0:T(8,128)}, f32[64,24,128]{2,1,0:T(8,128)}, u32[]{:S(2)}, u32[]{:S(2)}) collective-permute-start(f32[64,24,128]{2,1,0:T(8,128)} %get-tuple-element.49), channel_id=1, source_target_pairs={{0,4},{4,0},{8,12},{12,8},{16,20},{20,16},{24,28},{28,24},{1,5},{5... | collective-permute-start | bytes 2359304 | tf_op jit(solution)/shard_map/ppermute | solution.py:25
  67.4 59.4 %collective-permute-start.17 = (f32[64,24,128]{2,1,0:T(8,128)S(1)}, f32[64,24,128]{2,1,0:T(8,128)}, u32[]{:S(2)}, u32[]{:S(2)}) collective-permute-start(f32[64,24,128]{2,1,0:T(8,128)S(1)} %get-tuple-element.50.x_ref.rest_0_), channel_id=1, source_target_pairs={{0,8},{4,28},{8,16},{12,4},{16,24},{20,12},{24,0},{28,20},{1,9},{5... | collective-permute-start | bytes 2359304 | tf_op jit(solution)/shard_map/ppermute | solution.py:34
  69.4 2.4 %copy-start.4 = (f32[384,384]{1,0:T(8,128)S(1)}, f32[384,384]{1,0:T(8,128)}, u32[]{:S(2)}) copy-start(f32[384,384]{1,0:T(8,128)} %odd_ref.1) | copy-start | bytes 1769476
  69.4 2.4 %copy-start.7 = (f32[192,192]{1,0:T(8,128)S(1)}, f32[192,192]{1,0:T(8,128)}, u32[]{:S(2)}) copy-start(f32[192,192]{1,0:T(8,128)} %inv_ref.1) | copy-start | bytes 442372
  69.4 3.4 %copy-start.11 = (f32[64,24,128]{2,1,0:T(8,128)S(1)}, f32[64,24,128]{2,1,0:T(8,128)}, u32[]{:S(2)}) copy-start(f32[64,24,128]{2,1,0:T(8,128)} %copy-done.10) | copy-start | bytes 2359300
  72.8 3.6 %copy-start.9 = (f32[64,24,128]{2,1,0:T(8,128)S(1)}, f32[64,24,128]{2,1,0:T(8,128)}, u32[]{:S(2)}) copy-start(f32[64,24,128]{2,1,0:T(8,128)} %copy-done.8) | copy-start | bytes 2359300
  86.1 64.0 %copy-start.6 = (f32[2,512,128]{2,1,0:T(8,128)S(1)}, f32[2,512,128]{2,1,0:T(8,128)}, u32[]{:S(2)}) copy-start(f32[2,512,128]{2,1,0:T(8,128)} %copy-done.5) | copy-start | bytes 1572868
  86.1 45.6 %collective-permute-start.7 = (f32[64,24,128]{2,1,0:T(8,128)S(1)}, f32[64,24,128]{2,1,0:T(8,128)S(1)}, u32[]{:S(2)}, u32[]{:S(2)}) collective-permute-start(f32[64,24,128]{2,1,0:T(8,128)S(1)} %get-tuple-element.44.x_ref.rest_0_), channel_id=1, source_target_pairs={{0,24},{4,12},{8,0},{12,20},{16,8},{20,28},{24,16},{28,4},{1,25},{... | collective-permute-start | bytes 2359304 | tf_op jit(solution)/shard_map/ppermute | solution.py:34
  129.7 20.4 %collective-permute-start.20 = (f32[64,24,128]{2,1,0:T(8,128)S(1)}, f32[64,24,128]{2,1,0:T(8,128)S(1)}, u32[]{:S(2)}, u32[]{:S(2)}) collective-permute-start(f32[64,24,128]{2,1,0:T(8,128)S(1)} %get-tuple-element.55.x_ref.rest_0_), channel_id=1, source_target_pairs={{0,2},{1,3},{2,0},{3,1},{4,6},{5,7},{6,4},{7,5},{8,10},{9,11},{10,... | collective-permute-start | bytes 2359304 | tf_op jit(solution)/shard_map/ppermute | solution.py:20
  130.2 19.9 %collective-permute-start.18 = (f32[64,24,128]{2,1,0:T(8,128)S(1)}, f32[64,24,128]{2,1,0:T(8,128)S(1)}, u32[]{:S(2)}, u32[]{:S(2)}) collective-permute-start(f32[64,24,128]{2,1,0:T(8,128)S(1)} %get-tuple-element.55.x_ref.rest_0_), channel_id=1, source_target_pairs={{0,24},{4,12},{8,0},{12,20},{16,8},{20,28},{24,16},{28,4},{1,25},{... | collective-permute-start | bytes 2359304 | tf_op jit(solution)/shard_map/ppermute | solution.py:34
  130.2 22.6 %collective-permute-start.19 = (f32[64,24,128]{2,1,0:T(8,128)S(1)}, f32[64,24,128]{2,1,0:T(8,128)S(1)}, u32[]{:S(2)}, u32[]{:S(2)}) collective-permute-start(f32[64,24,128]{2,1,0:T(8,128)S(1)} %get-tuple-element.55.x_ref.rest_0_), channel_id=1, source_target_pairs={{0,1},{1,0},{2,3},{3,2},{4,5},{5,4},{6,7},{7,6},{8,9},{9,8},{10,11... | collective-permute-start | bytes 2359304 | tf_op jit(solution)/shard_map/ppermute | solution.py:20
  130.2 28.3 %collective-permute-start.9 = (f32[64,24,128]{2,1,0:T(8,128)S(1)}, f32[64,24,128]{2,1,0:T(8,128)S(1)}, u32[]{:S(2)}, u32[]{:S(2)}) collective-permute-start(f32[64,24,128]{2,1,0:T(8,128)S(1)} %get-tuple-element.44.x_ref.rest_0_), channel_id=1, source_target_pairs={{0,2},{1,3},{2,0},{3,1},{4,6},{5,7},{6,4},{7,5},{8,10},{9,11},{10,... | collective-permute-start | bytes 2359304 | tf_op jit(solution)/shard_map/ppermute | solution.py:20
  131.7 29.4 %collective-permute-start.23 = (f32[64,24,128]{2,1,0:T(8,128)S(1)}, f32[64,24,128]{2,1,0:T(8,128)S(1)}, u32[]{:S(2)}, u32[]{:S(2)}) collective-permute-start(f32[64,24,128]{2,1,0:T(8,128)S(1)} %get-tuple-element.55.x_ref.rest_0_), channel_id=1, source_target_pairs={{0,8},{4,28},{8,16},{12,4},{16,24},{20,12},{24,0},{28,20},{1,9},{5... | collective-permute-start | bytes 2359304 | tf_op jit(solution)/shard_map/ppermute | solution.py:34
  150.0 11.4 %collective-permute-start.21 = (f32[64,24,128]{2,1,0:T(8,128)S(1)}, f32[64,24,128]{2,1,0:T(8,128)S(1)}, u32[]{:S(2)}, u32[]{:S(2)}) collective-permute-start(f32[64,24,128]{2,1,0:T(8,128)S(1)} %collective-permute-done.20.rest_2_), channel_id=1, source_target_pairs={{0,1},{1,0},{2,3},{3,2},{4,5},{5,4},{6,7},{7,6},{8,9},{9,8},{10,11... | collective-permute-start | bytes 2359304 | tf_op jit(solution)/shard_map/ppermute | solution.py:20
  152.7 20.5 %collective-permute-start.22 = (f32[64,24,128]{2,1,0:T(8,128)S(1)}, f32[64,24,128]{2,1,0:T(8,128)S(1)}, u32[]{:S(2)}, u32[]{:S(2)}) collective-permute-start(f32[64,24,128]{2,1,0:T(8,128)S(1)} %get-tuple-element.54), channel_id=1, source_target_pairs={{0,4},{4,0},{8,12},{12,8},{16,20},{20,16},{24,28},{28,24},{1,5},{5... | collective-permute-start | bytes 2359304 | tf_op jit(solution)/shard_map/ppermute | solution.py:25
  152.7 22.1 %collective-permute-start.8 = (f32[64,24,128]{2,1,0:T(8,128)S(1)}, f32[64,24,128]{2,1,0:T(8,128)S(1)}, u32[]{:S(2)}, u32[]{:S(2)}) collective-permute-start(f32[64,24,128]{2,1,0:T(8,128)S(1)} %get-tuple-element.44.x_ref.rest_0_), channel_id=1, source_target_pairs={{0,1},{1,0},{2,3},{3,2},{4,5},{5,4},{6,7},{7,6},{8,9},{9,8},{10,11... | collective-permute-start | bytes 2359304 | tf_op jit(solution)/shard_map/ppermute | solution.py:20
  158.5 16.4 %collective-permute-start.10 = (f32[64,24,128]{2,1,0:T(8,128)S(1)}, f32[64,24,128]{2,1,0:T(8,128)S(1)}, u32[]{:S(2)}, u32[]{:S(2)}) collective-permute-start(f32[64,24,128]{2,1,0:T(8,128)S(1)} %collective-permute-done.9.rest_2_), channel_id=1, source_target_pairs={{0,1},{1,0},{2,3},{3,2},{4,5},{5,4},{6,7},{7,6},{8,9},{9,8},{10,11... | collective-permute-start | bytes 2359304 | tf_op jit(solution)/shard_map/ppermute | solution.py:20
  161.1 20.2 %collective-permute-start.12 = (f32[64,24,128]{2,1,0:T(8,128)S(1)}, f32[64,24,128]{2,1,0:T(8,128)S(1)}, u32[]{:S(2)}, u32[]{:S(2)}) collective-permute-start(f32[64,24,128]{2,1,0:T(8,128)S(1)} %get-tuple-element.44.x_ref.rest_0_), channel_id=1, source_target_pairs={{0,8},{4,28},{8,16},{12,4},{16,24},{20,12},{24,0},{28,20},{1,9},{5... | collective-permute-start | bytes 2359304 | tf_op jit(solution)/shard_map/ppermute | solution.py:34
  161.4 28.1 %collective-permute-start.11 = (f32[64,24,128]{2,1,0:T(8,128)S(1)}, f32[64,24,128]{2,1,0:T(8,128)S(1)}, u32[]{:S(2)}, u32[]{:S(2)}) collective-permute-start(f32[64,24,128]{2,1,0:T(8,128)S(1)} %get-tuple-element.43), channel_id=1, source_target_pairs={{0,4},{4,0},{8,12},{12,8},{16,20},{20,16},{24,28},{28,24},{1,5},{5... | collective-permute-start | bytes 2359304 | tf_op jit(solution)/shard_map/ppermute | solution.py:25
